TPU v7x, 32 devices: a whole 2x2x4 slice. The times are simulated.
32 devices in a mesh: survey: 2 (over y), band: 4 (over z), role: 4 (over x, core).
Axes of the slice: x: 2, y: 2, z: 4, core: 2. Of those that a mesh axis runs over, the one named last changes fastest.
Arguments:
- vel_index: int32 [16, 32, 128], P('role', 'band'), may hold values from 0 to 31
- courant: float32 [32], replicated, may hold values from 0.05 to 0.19
- src_now: float32 [32, 32, 128], P(('survey', 'role'), 'band'), parts along dimension 0, may hold values from -4 to 4
- src_prev: float32 [32, 32, 128], P(('survey', 'role'), 'band'), parts along dimension 0, may hold values from -4 to 4
- rec_now: float32 [32, 32, 128], P(('survey', 'role'), 'band'), parts along dimension 0, may hold values from -4 to 4
- rec_prev: float32 [32, 32, 128], P(('survey', 'role'), 'band'), parts along dimension 0, may hold values from -4 to 4
- src_pos: int32 [8, 3], P('survey'), parts along dimension 0, may hold values from 0 to 127, as said below
- src_wavelet: float32 [8, 16], P('survey'), parts along dimension 0, may hold values from -16 to 16
- rec_pos: int32 [8192, 2], P('survey'), parts along dimension 0, may hold values from 0 to 127, as said below
- rec_traces: float32 [8192, 16], P('survey'), parts along dimension 0, may hold values from -16 to 16
- offset_lags: int32 [32], replicated, may hold values from -16 to 16, as said below
Outputs:
- image: bfloat16 [64, 16, 32, 128], P('survey', 'role', 'band'), parts along dimension 0
- src_final: float32 [32, 32, 128], P(('survey', 'role'), 'band'), parts along dimension 0
- rec_final: float32 [32, 32, 128], P(('survey', 'role'), 'band'), parts along dimension 0
There are 2 independent parts, one for each index of `survey`. A program takes and returns all parts, laid end to end along the dimension named above; an argument that names none is the same for every part. Nothing has to cross between parts.
Inputs may be any that keep to these rules, and one draw needn't show every extreme that they name: `src_pos`: column 0 is a depth cell below 16, column 1 a cross-line cell below 32, column 2 an inline cell below 128; sources may share cells. `rec_pos`: column 0 is a cross-line cell below 32, column 1 an inline cell below 128; receivers may share cells. `offset_lags`: increasing and distinct: every whole number from -16 to 16 except one of the interior ones.
All inputs are finite; a program needn't handle non-finite values.
Results may differ from a plain program's by a relative error of at most 0.004.
Values may be sent and summed in bfloat16 or wider, within the bound.
No kernel may reach another device: no remote copies, remote signals or barrier semaphores. Data moves between devices by JAX's collectives and lax.ppermute only.
A program may use at most 128 MiB of HBM per device.

v0:
```python
import jax
import jax.numpy as jnp
from jax import lax
from jax.sharding import PartitionSpec as P

SUB = 4
IMAGES = 4


STENCIL_WEIGHTS = (-205.0 / 72.0, 8.0 / 5.0, -1.0 / 5.0, 8.0 / 315.0, -1.0 / 560.0)


def padded_2(block, sides, width):
    for axis, dim in sides:
        count = lax.axis_size(axis)
        forward = [(i, i + 1) for i in range(count - 1)]
        backward = [(target, source) for source, target in forward]
        low = lax.ppermute(
            lax.slice_in_dim(block, block.shape[dim] - width, None, axis=dim), axis, forward
        )
        high = lax.ppermute(lax.slice_in_dim(block, 0, width, axis=dim), axis, backward)
        block = jnp.concatenate([low, block, high], axis=dim)
    return block


def laplace(padded, depth_cells, row_cells, col_cells):

    def window(along_z, along_y, along_x):
        return padded[
            :,
            4 + along_z : 4 + along_z + depth_cells,
            4 + along_y : 4 + along_y + row_cells,
            4 + along_x : 4 + along_x + col_cells,
        ]

    summed = 3.0 * STENCIL_WEIGHTS[0] * window(0, 0, 0)
    for distance in range(1, 5):
        weight = STENCIL_WEIGHTS[distance]
        pairs = window(distance, 0, 0) + window(-distance, 0, 0)
        pairs = pairs + window(0, distance, 0) + window(0, -distance, 0)
        pairs = pairs + window(0, 0, distance) + window(0, 0, -distance)
        summed = summed + weight * pairs
    return summed


def lookup(vel_index, courant):
    levels = courant.shape[0]

    def add_level(level, summed):
        return summed + jnp.where(vel_index == level, courant[level], 0.0)

    return lax.fori_loop(0, levels, add_level, jnp.zeros(vel_index.shape, jnp.float32))


def local_index(global_at, start, extent):
    local_at = global_at - start
    inside = (local_at >= 0) & (local_at < extent)
    return jnp.where(inside, local_at, extent)


def inject_all(shape, depth_at, row_at, col_at, amounts):
    step_count = amounts.shape[1]
    return (
        jnp.zeros((step_count,) + shape, jnp.float32)
        .at[:, depth_at, row_at, col_at]
        .add(amounts.T, mode="drop")
    )


def lag_products(source_pad, receiver_pad, offset_lags, max_lag, col_cells):

    def product(lag_value):
        src_part = lax.dynamic_slice_in_dim(source_pad, max_lag - lag_value, col_cells, 2)
        rec_part = lax.dynamic_slice_in_dim(receiver_pad, max_lag + lag_value, col_cells, 2)
        return src_part * rec_part

    return jax.vmap(product)(offset_lags)


def depth_filter(padded, depth_cells):
    return (
        2.0 * padded[:, 1 : 1 + depth_cells]
        - padded[:, 0:depth_cells]
        - padded[:, 2 : 2 + depth_cells]
    )


def pad_inline(state, max_lag):
    return jnp.pad(state, ((0, 0), (0, 0), (0, 0), (max_lag, max_lag)))


def accumulate(slab_state, image_sum, edge_sum, offset_lags, max_lag):
    col_cells = slab_state.shape[3]
    padded = pad_inline(slab_state, max_lag)
    image_sum = image_sum + lag_products(padded[0], padded[1], offset_lags, max_lag, col_cells)
    return (image_sum, edge_sum)


def finish(image_sum):
    padded = padded_2(image_sum, (("role", 1),), 1)
    return depth_filter(padded, image_sum.shape[1]).astype(jnp.bfloat16)


def shards(
    vel_index,
    courant,
    src_now,
    src_prev,
    rec_now,
    rec_prev,
    src_pos,
    src_wavelet,
    rec_pos,
    rec_traces,
    offset_lags,
):
    lag_count = offset_lags.shape[0]
    max_lag = lag_count // 2
    speed = lookup(vel_index, courant)
    band_start = lax.axis_index("band") * src_now.shape[1]
    role_at = lax.axis_index("role")
    current = jnp.stack([src_now, rec_now])
    previous = jnp.stack([src_prev, rec_prev])
    depth_start = role_at * src_now.shape[0]
    col_start = 0

    def faces(state):
        padded = padded_2(state, (("band", 2), ("role", 1)), 4)
        return jnp.pad(padded, ((0, 0), (0, 0), (0, 0), (4, 4)))

    depth_cells, row_cells, col_cells = speed.shape
    shape = speed.shape
    slab_shape = src_now.shape
    src_depth = local_index(src_pos[:, 0], depth_start, depth_cells)
    src_row = local_index(src_pos[:, 1], band_start, row_cells)
    src_col = local_index(src_pos[:, 2], col_start, col_cells)
    rec_depth = local_index(jnp.zeros_like(rec_pos[:, 0]), depth_start, depth_cells)
    rec_row = local_index(rec_pos[:, 0], band_start, row_cells)
    rec_col = local_index(rec_pos[:, 1], col_start, col_cells)
    src_terms = inject_all(shape, src_depth, src_row, src_col, src_wavelet)
    rec_terms = inject_all(shape, rec_depth, rec_row, rec_col, rec_traces)
    image_sum = jnp.zeros((lag_count,) + slab_shape, jnp.float32)
    edge_sum = jnp.zeros((lag_count, 2) + slab_shape[1:], jnp.float32)
    slab_state = current
    for snapshot in range(IMAGES):

        def advance(substep, carry):
            state, older = carry
            tick_at = snapshot * SUB + substep
            sources = jnp.stack(
                [
                    lax.dynamic_index_in_dim(src_terms, tick_at, 0, keepdims=False),
                    lax.dynamic_index_in_dim(rec_terms, tick_at, 0, keepdims=False),
                ]
            )
            laplacian = laplace(faces(state), depth_cells, row_cells, col_cells)
            updated = 2.0 * state - older + speed * (laplacian + sources)
            return (updated, state)

        current, previous = lax.fori_loop(0, SUB, advance, (current, previous))
        slab_state = current
        image_sum, edge_sum = accumulate(slab_state, image_sum, edge_sum, offset_lags, max_lag)
    image = finish(image_sum)
    return (image, slab_state[0], slab_state[1])


def solution(mesh):
    placed = (
        P("role", "band", None),
        P(),
        P(("survey", "role"), "band", None),
        P(("survey", "role"), "band", None),
        P(("survey", "role"), "band", None),
        P(("survey", "role"), "band", None),
        P("survey", None),
        P("survey", None),
        P("survey", None),
        P("survey", None),
        P(),
    )
    return jax.shard_map(
        shards,
        mesh=mesh,
        in_specs=placed,
        out_specs=(
            P("survey", "role", "band", None),
            P(("survey", "role"), "band", None),
            P(("survey", "role"), "band", None),
        ),
        check_vma=False,
    )
```

profile of v0, /device:TPU:0, one launch (start us, length us, event | category | flops | bytes accessed | tf_op | source)
XLA Modules:
  0.0 502.1 jit_solution(1492529173668572404)
XLA Ops:
  0.7 83.2 %while.86 = (s32[]{:T(128)}, f32[4,8,128]{2,1,0:T(8,128)S(1)}, s32[4,8,128]{2,1,0:T(8,128)}, f32[32]{0:T(128)}, s32[]{:T(128)}, /*index=5*/s32[]{:T(128)}) while((s32[]{:T(128)}, f32[4,8,128]{2,1,0:T(8,128)S(1)}, s32[4,8,128]{2,1,0:T(8,128)}, f32[32]{0:T(128)}, s32[]{:T(128)}, /*index=5*/s32[]{:T(128)}) %tuple.207), condition=%wide.region_3.4_spmd.clone, body=%wide.region_2.3_spmd.clone.sunk | while | flops 16387 | bytes 49259 | solution.py:52
  90.3 23.3 %scatter_custom_fusion.1 = f32[16,4096]{0,1:T(8,128)S(1)} fusion(s32[4096]{0:T(1024)S(1)} %broadcast_select_fusion, f32[4096,16]{1,0:T(8,128)} %copy.49, f32[]{:T(128)} %constant.463.clone.1), kind=kCustom, calls=%fused_computation.247 | custom fusion | flops 65536 | bytes 262656
  116.0 66.7 %while.82 = (s32[]{:T(128)}, f32[2,4,8,128]{3,2,1,0:T(8,128)S(1)}, f32[2,4,8,128]{3,2,1,0:T(8,128)S(1)}, f32[4,8,128]{2,1,0:T(8,128)S(1)}, f32[16,4,8,128]{3,2,1...) while((s32[]{:T(128)}, f32[2,4,8,128]{3,2,1,0:T(8,128)S(1)}, f32[2,4,8,128]{3,2,1,0:T(8,128)S(1)}, ...), condition=%wide.region_5.6_spmd, body=%wide.region_4.5_spmd.sunk | while | flops 1126402 | bytes 2322673 | solution.py:160
  116.0 5.0 collective-permute-start
  182.7 61.8 %while.83 = (s32[]{:T(128)}, f32[2,4,8,128]{3,2,1,0:T(8,128)S(1)}, f32[2,4,8,128]{3,2,1,0:T(8,128)S(1)}, f32[4,8,128]{2,1,0:T(8,128)S(1)}, f32[16,4,8,128]{3,2,1...) while((s32[]{:T(128)}, f32[2,4,8,128]{3,2,1,0:T(8,128)S(1)}, ...), condition=%wide.region_7.8_spmd, body=%wide.region_6.7_spmd.sunk | while | flops 1126406 | bytes 2322743 | solution.py:160
  244.5 61.8 %while.84 = (s32[]{:T(128)}, f32[2,4,8,128]{3,2,1,0:T(8,128)S(1)}, f32[2,4,8,128]{3,2,1,0:T(8,128)S(1)}, f32[4,8,128]{2,1,0:T(8,128)S(1)}, f32[16,4,8,128]{3,2,1...) while((s32[]{:T(128)}, f32[2,4,8,128]{3,2,1,0:T(8,128)S(1)}, ...), condition=%wide.region_9.10_spmd, body=%wide.region_8.9_spmd.sunk | while | flops 1126406 | bytes 2322743 | solution.py:160
  308.4 61.8 %while.85 = (s32[]{:T(128)}, f32[2,4,8,128]{3,2,1,0:T(8,128)S(1)}, f32[2,4,8,128]{3,2,1,0:T(8,128)S(1)}, f32[4,8,128]{2,1,0:T(8,128)S(1)}, f32[16,4,8,128]{3,2,1...) while((s32[]{:T(128)}, f32[2,4,8,128]{3,2,1,0:T(8,128)S(1)}, ...), condition=%wide.region_11.12_spmd, body=%wide.region_10.11_spmd.sunk | while | flops 1126406 | bytes 2322743 | solution.py:160
  372.1 7.9 %gather_fusion.1 = f32[32,4,8,128]{2,1,3,0:T(4,128)} fusion(f32[4,8,160]{1,0,2:T(4,128)S(1)} %get-tuple-element.879, s32[32]{0:T(128)S(1)} %get-tuple-element.891), kind=kCustom, calls=%fused_computation.1 | custom fusion | bytes 1048960 | tf_op jit(solution)/shard_map/vmap()/gather | solution.py:74
  379.9 6.6 %copy.54 = f32[32,4,8,128]{3,2,1,0:T(8,128)S(1)} copy(f32[32,4,8,128]{2,1,3,0:T(4,128)} %gather_fusion.1) | data formatting | bytes 1048576 | tf_op jit(solution)/shard_map/vmap()/gather | solution.py:74
  386.5 7.9 %gather_fusion.3 = f32[32,4,8,128]{2,1,3,0:T(4,128)} fusion(f32[4,8,160]{1,0,2:T(4,128)S(1)} %get-tuple-element.881, s32[32]{0:T(128)S(1)} %get-tuple-element.891), kind=kCustom, calls=%fused_computation.3 | custom fusion | bytes 1048960 | tf_op jit(solution)/shard_map/vmap()/gather | solution.py:74
  394.4 6.6 %copy.59 = f32[32,4,8,128]{3,2,1,0:T(8,128)S(1)} copy(f32[32,4,8,128]{2,1,3,0:T(4,128)} %gather_fusion.3) | data formatting | bytes 1048576 | tf_op jit(solution)/shard_map/vmap()/gather | solution.py:74
  401.0 8.1 %gather_fusion.5 = f32[32,4,8,128]{2,1,3,0:T(4,128)} fusion(f32[4,8,160]{1,0,2:T(4,128)S(1)} %get-tuple-element.883, s32[32]{0:T(128)S(1)} %get-tuple-element.891), kind=kCustom, calls=%fused_computation.5 | custom fusion | bytes 1048960 | tf_op jit(solution)/shard_map/vmap()/gather | solution.py:74
  409.1 6.6 %copy.64 = f32[32,4,8,128]{3,2,1,0:T(8,128)S(1)} copy(f32[32,4,8,128]{2,1,3,0:T(4,128)} %gather_fusion.5) | data formatting | bytes 1048576 | tf_op jit(solution)/shard_map/vmap()/gather | solution.py:74
  415.7 7.9 %gather_fusion.7 = f32[32,4,8,128]{2,1,3,0:T(4,128)} fusion(f32[4,8,160]{1,0,2:T(4,128)S(1)} %get-tuple-element.885, s32[32]{0:T(128)S(1)} %get-tuple-element.891), kind=kCustom, calls=%fused_computation.7 | custom fusion | bytes 1048960 | tf_op jit(solution)/shard_map/vmap()/gather | solution.py:74
  423.5 7.4 %copy.69 = f32[32,4,8,128]{3,2,1,0:T(8,128)} copy(f32[32,4,8,128]{2,1,3,0:T(4,128)} %gather_fusion.7) | data formatting | bytes 1048576 | tf_op jit(solution)/shard_map/vmap()/gather | solution.py:74
  430.9 7.9 %gather_fusion = f32[32,4,8,128]{2,1,3,0:T(4,128)} fusion(f32[4,8,160]{1,0,2:T(4,128)S(1)} %get-tuple-element.880, s32[32]{0:T(128)S(1)} %get-tuple-element.892), kind=kCustom, calls=%fused_computation | custom fusion | bytes 1048960 | tf_op jit(solution)/shard_map/vmap()/gather | solution.py:73
  438.7 6.6 %copy.53 = f32[32,4,8,128]{3,2,1,0:T(8,128)S(1)} copy(f32[32,4,8,128]{2,1,3,0:T(4,128)} %gather_fusion) | data formatting | bytes 1048576 | tf_op jit(solution)/shard_map/vmap()/gather | solution.py:73
  445.3 7.9 %gather_fusion.2 = f32[32,4,8,128]{2,1,3,0:T(4,128)} fusion(f32[4,8,160]{1,0,2:T(4,128)S(1)} %get-tuple-element.882, s32[32]{0:T(128)S(1)} %get-tuple-element.892), kind=kCustom, calls=%fused_computation.2 | custom fusion | bytes 1048960 | tf_op jit(solution)/shard_map/vmap()/gather | solution.py:73
  453.2 7.4 %copy.58 = f32[32,4,8,128]{3,2,1,0:T(8,128)} copy(f32[32,4,8,128]{2,1,3,0:T(4,128)} %gather_fusion.2) | data formatting | bytes 1048576 | tf_op jit(solution)/shard_map/vmap()/gather | solution.py:73
  460.6 8.1 %gather_fusion.4 = f32[32,4,8,128]{2,1,3,0:T(4,128)} fusion(f32[4,8,160]{1,0,2:T(4,128)S(1)} %get-tuple-element.884, s32[32]{0:T(128)S(1)} %get-tuple-element.892), kind=kCustom, calls=%fused_computation.4 | custom fusion | bytes 1048960 | tf_op jit(solution)/shard_map/vmap()/gather | solution.py:73
  468.7 7.4 %copy.63 = f32[32,4,8,128]{3,2,1,0:T(8,128)} copy(f32[32,4,8,128]{2,1,3,0:T(4,128)} %gather_fusion.4) | data formatting | bytes 1048576 | tf_op jit(solution)/shard_map/vmap()/gather | solution.py:73
  476.1 7.9 %gather_fusion.6 = f32[32,4,8,128]{2,1,3,0:T(4,128)} fusion(f32[4,8,160]{1,0,2:T(4,128)S(1)} %get-tuple-element.886, s32[32]{0:T(128)S(1)} %get-tuple-element.892), kind=kCustom, calls=%fused_computation.6 | custom fusion | bytes 1048960 | tf_op jit(solution)/shard_map/vmap()/gather | solution.py:73
  483.9 7.4 %copy.68 = f32[32,4,8,128]{3,2,1,0:T(8,128)} copy(f32[32,4,8,128]{2,1,3,0:T(4,128)} %gather_fusion.6) | data formatting | bytes 1048576 | tf_op jit(solution)/shard_map/vmap()/gather | solution.py:73
  493.2 4.8 collective-permute-start.16
  (382 shorter events, 346.9 us)
Async XLA Ops:
  116.0 6.4 %collective-permute-start = (f32[2,4,4,128]{3,2,1,0:T(4,128)S(1)}, f32[2,4,4,128]{3,2,1,0:T(4,128)S(1)}, u32[]{:S(2)}, u32[]{:S(2)}) collective-permute-start(f32[2,4,4,128]{3,2,1,0:T(4,128)S(1)} %get-tuple-element.1062), channel_id=1, source_target_pairs={{0,4},{4,8},{8,12},{1,5},{5,9},{9,13},{2,6},{6,10},{10,14},{3,7},{... | collective-permute-start | bytes 49160 | tf_op jit(solution)/shard_map/while/body/eval_jaxpr/ppermute | solution.py:18
  121.0 5.6 %collective-permute-start.1 = (f32[2,4,4,128]{3,2,1,0:T(4,128)S(1)}, f32[2,4,4,128]{3,2,1,0:T(4,128)S(1)}, u32[]{:S(2)}, u32[]{:S(2)}) collective-permute-start(f32[2,4,4,128]{3,2,1,0:T(4,128)S(1)} %get-tuple-element.1063), channel_id=1, source_target_pairs={{4,0},{8,4},{12,8},{5,1},{9,5},{13,9},{6,2},{10,6},{14,10},{7,3},{... | collective-permute-start | bytes 49160 | tf_op jit(solution)/shard_map/while/body/eval_jaxpr/ppermute | solution.py:21
  127.9 4.9 collective-permute-start.2
  133.2 4.9 collective-permute-start
  136.7 5.6 %collective-permute-start.1 = (f32[2,4,4,128]{3,2,1,0:T(4,128)S(1)}, f32[2,4,4,128]{3,2,1,0:T(4,128)S(1)}, u32[]{:S(2)}, u32[]{:S(2)}) collective-permute-start(f32[2,4,4,128]{3,2,1,0:T(4,128)S(1)} %get-tuple-element.1063), channel_id=1, source_target_pairs={{4,0},{8,4},{12,8},{5,1},{9,5},{13,9},{6,2},{10,6},{14,10},{7,3},{... | collective-permute-start | bytes 49160 | tf_op jit(solution)/shard_map/while/body/eval_jaxpr/ppermute | solution.py:21
  150.2 4.9 collective-permute-start
  153.7 5.6 %collective-permute-start.1 = (f32[2,4,4,128]{3,2,1,0:T(4,128)S(1)}, f32[2,4,4,128]{3,2,1,0:T(4,128)S(1)}, u32[]{:S(2)}, u32[]{:S(2)}) collective-permute-start(f32[2,4,4,128]{3,2,1,0:T(4,128)S(1)} %get-tuple-element.1063), channel_id=1, source_target_pairs={{4,0},{8,4},{12,8},{5,1},{9,5},{13,9},{6,2},{10,6},{14,10},{7,3},{... | collective-permute-start | bytes 49160 | tf_op jit(solution)/shard_map/while/body/eval_jaxpr/ppermute | solution.py:21
  169.1 5.6 %collective-permute-start.1 = (f32[2,4,4,128]{3,2,1,0:T(4,128)S(1)}, f32[2,4,4,128]{3,2,1,0:T(4,128)S(1)}, u32[]{:S(2)}, u32[]{:S(2)}) collective-permute-start(f32[2,4,4,128]{3,2,1,0:T(4,128)S(1)} %get-tuple-element.1063), channel_id=1, source_target_pairs={{4,0},{8,4},{12,8},{5,1},{9,5},{13,9},{6,2},{10,6},{14,10},{7,3},{... | collective-permute-start | bytes 49160 | tf_op jit(solution)/shard_map/while/body/eval_jaxpr/ppermute | solution.py:21
  174.8 4.7 collective-permute-start.3
  184.6 5.6 %collective-permute-start.5 = (f32[2,4,4,128]{3,2,1,0:T(4,128)S(1)}, f32[2,4,4,128]{3,2,1,0:T(4,128)S(1)}, u32[]{:S(2)}, u32[]{:S(2)}) collective-permute-start(f32[2,4,4,128]{3,2,1,0:T(4,128)S(1)} %get-tuple-element.1073), channel_id=1, source_target_pairs={{4,0},{8,4},{12,8},{5,1},{9,5},{13,9},{6,2},{10,6},{14,10},{7,3},{... | collective-permute-start | bytes 49160 | tf_op jit(solution)/shard_map/while/body/eval_jaxpr/ppermute | solution.py:21
  200.1 5.6 %collective-permute-start.5 = (f32[2,4,4,128]{3,2,1,0:T(4,128)S(1)}, f32[2,4,4,128]{3,2,1,0:T(4,128)S(1)}, u32[]{:S(2)}, u32[]{:S(2)}) collective-permute-start(f32[2,4,4,128]{3,2,1,0:T(4,128)S(1)} %get-tuple-element.1073), channel_id=1, source_target_pairs={{4,0},{8,4},{12,8},{5,1},{9,5},{13,9},{6,2},{10,6},{14,10},{7,3},{... | collective-permute-start | bytes 49160 | tf_op jit(solution)/shard_map/while/body/eval_jaxpr/ppermute | solution.py:21
  215.5 5.6 %collective-permute-start.5 = (f32[2,4,4,128]{3,2,1,0:T(4,128)S(1)}, f32[2,4,4,128]{3,2,1,0:T(4,128)S(1)}, u32[]{:S(2)}, u32[]{:S(2)}) collective-permute-start(f32[2,4,4,128]{3,2,1,0:T(4,128)S(1)} %get-tuple-element.1073), channel_id=1, source_target_pairs={{4,0},{8,4},{12,8},{5,1},{9,5},{13,9},{6,2},{10,6},{14,10},{7,3},{... | collective-permute-start | bytes 49160 | tf_op jit(solution)/shard_map/while/body/eval_jaxpr/ppermute | solution.py:21
  230.9 5.6 %collective-permute-start.5 = (f32[2,4,4,128]{3,2,1,0:T(4,128)S(1)}, f32[2,4,4,128]{3,2,1,0:T(4,128)S(1)}, u32[]{:S(2)}, u32[]{:S(2)}) collective-permute-start(f32[2,4,4,128]{3,2,1,0:T(4,128)S(1)} %get-tuple-element.1073), channel_id=1, source_target_pairs={{4,0},{8,4},{12,8},{5,1},{9,5},{13,9},{6,2},{10,6},{14,10},{7,3},{... | collective-permute-start | bytes 49160 | tf_op jit(solution)/shard_map/while/body/eval_jaxpr/ppermute | solution.py:21
  246.4 5.6 %collective-permute-start.9 = (f32[2,4,4,128]{3,2,1,0:T(4,128)S(1)}, f32[2,4,4,128]{3,2,1,0:T(4,128)S(1)}, u32[]{:S(2)}, u32[]{:S(2)}) collective-permute-start(f32[2,4,4,128]{3,2,1,0:T(4,128)S(1)} %get-tuple-element.1083), channel_id=1, source_target_pairs={{4,0},{8,4},{12,8},{5,1},{9,5},{13,9},{6,2},{10,6},{14,10},{7,3},{... | collective-permute-start | bytes 49160 | tf_op jit(solution)/shard_map/while/body/eval_jaxpr/ppermute | solution.py:21
  261.9 5.6 %collective-permute-start.9 = (f32[2,4,4,128]{3,2,1,0:T(4,128)S(1)}, f32[2,4,4,128]{3,2,1,0:T(4,128)S(1)}, u32[]{:S(2)}, u32[]{:S(2)}) collective-permute-start(f32[2,4,4,128]{3,2,1,0:T(4,128)S(1)} %get-tuple-element.1083), channel_id=1, source_target_pairs={{4,0},{8,4},{12,8},{5,1},{9,5},{13,9},{6,2},{10,6},{14,10},{7,3},{... | collective-permute-start | bytes 49160 | tf_op jit(solution)/shard_map/while/body/eval_jaxpr/ppermute | solution.py:21
  267.5 4.7 collective-permute-start.11
  277.3 5.6 %collective-permute-start.9 = (f32[2,4,4,128]{3,2,1,0:T(4,128)S(1)}, f32[2,4,4,128]{3,2,1,0:T(4,128)S(1)}, u32[]{:S(2)}, u32[]{:S(2)}) collective-permute-start(f32[2,4,4,128]{3,2,1,0:T(4,128)S(1)} %get-tuple-element.1083), channel_id=1, source_target_pairs={{4,0},{8,4},{12,8},{5,1},{9,5},{13,9},{6,2},{10,6},{14,10},{7,3},{... | collective-permute-start | bytes 49160 | tf_op jit(solution)/shard_map/while/body/eval_jaxpr/ppermute | solution.py:21
  292.7 5.6 %collective-permute-start.9 = (f32[2,4,4,128]{3,2,1,0:T(4,128)S(1)}, f32[2,4,4,128]{3,2,1,0:T(4,128)S(1)}, u32[]{:S(2)}, u32[]{:S(2)}) collective-permute-start(f32[2,4,4,128]{3,2,1,0:T(4,128)S(1)} %get-tuple-element.1083), channel_id=1, source_target_pairs={{4,0},{8,4},{12,8},{5,1},{9,5},{13,9},{6,2},{10,6},{14,10},{7,3},{... | collective-permute-start | bytes 49160 | tf_op jit(solution)/shard_map/while/body/eval_jaxpr/ppermute | solution.py:21
  298.4 4.7 collective-permute-start.11
  310.4 5.6 %collective-permute-start.13 = (f32[2,4,4,128]{3,2,1,0:T(4,128)S(1)}, f32[2,4,4,128]{3,2,1,0:T(4,128)S(1)}, u32[]{:S(2)}, u32[]{:S(2)}) collective-permute-start(f32[2,4,4,128]{3,2,1,0:T(4,128)S(1)} %get-tuple-element.1093), channel_id=1, source_target_pairs={{4,0},{8,4},{12,8},{5,1},{9,5},{13,9},{6,2},{10,6},{14,10},{7,3},{... | collective-permute-start | bytes 49160 | tf_op jit(solution)/shard_map/while/body/eval_jaxpr/ppermute | solution.py:21
  325.8 5.6 %collective-permute-start.13 = (f32[2,4,4,128]{3,2,1,0:T(4,128)S(1)}, f32[2,4,4,128]{3,2,1,0:T(4,128)S(1)}, u32[]{:S(2)}, u32[]{:S(2)}) collective-permute-start(f32[2,4,4,128]{3,2,1,0:T(4,128)S(1)} %get-tuple-element.1093), channel_id=1, source_target_pairs={{4,0},{8,4},{12,8},{5,1},{9,5},{13,9},{6,2},{10,6},{14,10},{7,3},{... | collective-permute-start | bytes 49160 | tf_op jit(solution)/shard_map/while/body/eval_jaxpr/ppermute | solution.py:21
  341.3 5.6 %collective-permute-start.13 = (f32[2,4,4,128]{3,2,1,0:T(4,128)S(1)}, f32[2,4,4,128]{3,2,1,0:T(4,128)S(1)}, u32[]{:S(2)}, u32[]{:S(2)}) collective-permute-start(f32[2,4,4,128]{3,2,1,0:T(4,128)S(1)} %get-tuple-element.1093), channel_id=1, source_target_pairs={{4,0},{8,4},{12,8},{5,1},{9,5},{13,9},{6,2},{10,6},{14,10},{7,3},{... | collective-permute-start | bytes 49160 | tf_op jit(solution)/shard_map/while/body/eval_jaxpr/ppermute | solution.py:21
  356.7 5.6 %collective-permute-start.13 = (f32[2,4,4,128]{3,2,1,0:T(4,128)S(1)}, f32[2,4,4,128]{3,2,1,0:T(4,128)S(1)}, u32[]{:S(2)}, u32[]{:S(2)}) collective-permute-start(f32[2,4,4,128]{3,2,1,0:T(4,128)S(1)} %get-tuple-element.1093), channel_id=1, source_target_pairs={{4,0},{8,4},{12,8},{5,1},{9,5},{13,9},{6,2},{10,6},{14,10},{7,3},{... | collective-permute-start | bytes 49160 | tf_op jit(solution)/shard_map/while/body/eval_jaxpr/ppermute | solution.py:21
  493.2 6.8 %collective-permute-start.16 = (f32[32,1,8,128]{3,2,1,0:T(8,128)S(1)}, f32[32,1,8,128]{3,2,1,0:T(8,128)S(1)}, u32[]{:S(2)}, u32[]{:S(2)}) collective-permute-start(f32[32,1,8,128]{3,2,1,0:T(8,128)S(1)} %get-tuple-element.877), channel_id=1, source_target_pairs={{0,1},{1,2},{2,3},{4,5},{5,6},{6,7},{8,9},{9,10},{10,11},{12,13},{... | collective-permute-start | bytes 393224 | tf_op jit(solution)/shard_map/ppermute | solution.py:18
  (50 other events, 893.5 us)
where the time goes:
time: 510 us; the launch traced here: 502 us
  local copies, waits for them, and re-layouts  172 us (34%)
  starting transfers between devices  137 us (27%)
  waiting for transfers between devices  112 us (22%)
  other arithmetic  78.5 us (15%)
    ppermute x33, waiting for transfers between devices, padded_2(): lax.ppermute(lax.slice_in_dim(block, 0, width, axis=dim), axis, backward)  110 us
    ppermute x33, starting transfers between devices, padded_2(): lax.ppermute(lax.slice_in_dim(block, block.shape[dim] - width, None, axis...  94.2 us
    gather x8, local copies, waits for them, and re-layouts, product(): lax.dynamic_slice_in_dim(source_pad, max_lag - lag_value, col_cells, 2)  60.4 us
    gather x8, local copies, waits for them, and re-layouts, product(): lax.dynamic_slice_in_dim(receiver_pad, max_lag + lag_value, col_cells, 2)  58.8 us
    ppermute x33, starting transfers between devices, padded_2(): lax.ppermute(lax.slice_in_dim(block, 0, width, axis=dim), axis, backward)  42.6 us
    add x32, other arithmetic, add_level(): return summed + jnp.where(vel_index == level, courant[level], 0.0)  42.5 us
    dynamic_slice x32, local copies, waits for them, and re-layouts, add_level(): return summed + jnp.where(vel_index == level, courant[level], 0.0)  40.6 us
    unnamed x5, other arithmetic  24.9 us
  transfers between devices with their start and end apart: 66, of which 45 were waited for; matrix products, arithmetic and copies ran while one was open for 1% of the time, Pallas kernels for 0%

commit v1 on v0

v1 whole, which is shorter than its diff:
```python
import functools

import jax
import jax.numpy as jnp
from jax import lax
from jax.experimental import pallas as pl
from jax.experimental.pallas import tpu as pltpu
from jax.sharding import PartitionSpec as P

SUB = 4
IMAGES = 4
PARTS = 5
CORES = 2

STENCIL_WEIGHTS = (-205.0 / 72.0, 8.0 / 5.0, -1.0 / 5.0, 8.0 / 315.0, -1.0 / 560.0)
F32 = jnp.float32
BF16 = jnp.bfloat16

VMEM_SPEC = pl.BlockSpec(memory_space=pltpu.VMEM)
SMEM_SPEC = pl.BlockSpec(memory_space=pltpu.SMEM)


def split(value):
    high = value.astype(BF16)
    return high, (value - high.astype(F32)).astype(BF16)


def pack_kernel(vel_ref, sn_ref, sp_ref, rn_ref, rp_ref, keep_ref, send_ref):
    core = lax.rem(lax.axis_index("role"), CORES)
    entry = vel_ref[...].astype(F32).astype(BF16)
    src_now, rec_now = sn_ref[...], rn_ref[...]
    src_step, rec_step = src_now - sp_ref[...], rec_now - rp_ref[...]
    for out_ref, wants_source in ((keep_ref, core == 0), (send_ref, core != 0)):
        now = jnp.where(wants_source, src_now, rec_now)
        step = jnp.where(wants_source, src_step, rec_step)
        out_ref[0], out_ref[1] = split(now)
        out_ref[2], out_ref[3] = split(step)
        out_ref[4] = entry


def pack(vel_index, src_now, src_prev, rec_now, rec_prev):
    shape = jax.ShapeDtypeStruct((PARTS,) + src_now.shape, BF16)
    return pl.pallas_call(
        pack_kernel,
        out_shape=(shape, shape),
        in_specs=[VMEM_SPEC] * 5,
        out_specs=(VMEM_SPEC, VMEM_SPEC),
        name="pack",
    )(vel_index, src_now, src_prev, rec_now, rec_prev)


def inject_kernel(chunk, pos_ref, amp_ref, out_ref, acc_ref):
    steps, count = amp_ref.shape
    _, rows, cols = out_ref.shape
    acc_ref[...] = jnp.zeros_like(acc_ref)

    def one(at, carry):
        span = pl.ds(pl.multiple_of(at * chunk, chunk), chunk)
        pos = pos_ref[:, span]
        in_row = lax.broadcasted_iota(jnp.int32, (rows, chunk), 0) == pos[0:1]
        in_col = lax.broadcasted_iota(jnp.int32, (cols, chunk), 0) == pos[1:2]
        col_hot = jnp.where(in_col, 1.0, 0.0).astype(BF16)
        amp = amp_ref[:, span]
        high = amp.astype(BF16).astype(F32)
        total = None
        for part in (high, amp - high):
            spread = jnp.concatenate(
                [jnp.where(in_row, part[k : k + 1], 0.0).astype(BF16) for k in range(steps)], axis=0
            )
            added = lax.dot_general(
                spread, col_hot, (((1,), (1,)), ((), ())), preferred_element_type=F32
            )
            total = added if total is None else total + added
        acc_ref[...] += total
        return carry

    lax.fori_loop(0, count // chunk, one, 0)
    for k in range(steps):
        out_ref[k] = acc_ref[k * rows : (k + 1) * rows]


def inject(rec_pos, rec_traces, rows, cols):
    count, steps = rec_traces.shape
    chunk = next(c for c in (512, 256, 128, count) if count % c == 0)
    return pl.pallas_call(
        functools.partial(inject_kernel, chunk),
        out_shape=jax.ShapeDtypeStruct((steps, rows, cols), F32),
        in_specs=[VMEM_SPEC] * 2,
        out_specs=VMEM_SPEC,
        scratch_shapes=[pltpu.VMEM((steps * rows, cols), F32)],
        name="inject",
    )(rec_pos.T, rec_traces.T)


def lookup(table, entry):
    width = table.shape[1]
    pieces = [
        jnp.take_along_axis(table, entry[:, at : at + width], axis=1)
        for at in range(0, entry.shape[1], width)
    ]
    return pieces[0] if len(pieces) == 1 else jnp.concatenate(pieces, axis=1)


def step_kernel(bands, chips, steps, *refs):
    wavelet_ref, src_pos_ref, table_ref, added_ref = refs[:4]
    piece_refs = refs[4 : 4 + bands * chips]
    keep_ref, send_ref, one_ref, two_ref, speed_ref, row_ref = refs[4 + bands * chips :]
    _, _, tile_z, tile_y, cols = piece_refs[0].shape
    depth, rows, _ = speed_ref.shape
    role, band = lax.axis_index("role"), lax.axis_index("band")
    core, chip = lax.rem(role, CORES), lax.div(role, CORES)
    is_source = core == 0
    sources = src_pos_ref.shape[0]

    for ref in (one_ref, two_ref):
        edge = jnp.zeros((rows + 16, cols), F32)
        ref[0] = edge
        ref[depth + 1] = edge
        for z in range(1, depth + 1):
            ref[z, 0:8] = edge[0:8]
            ref[z, rows + 8 :] = edge[0:8]

    table = jnp.broadcast_to(table_ref[...], (tile_y, table_ref.shape[1]))
    for shift in range(bands):
        from_band = lax.rem(band + (bands - shift), bands)
        y0 = pl.multiple_of(from_band * tile_y, tile_y)
        for hop in range(chips):
            from_chip = lax.rem(chip + (chips - hop), chips)
            piece = piece_refs[shift * chips + hop]
            for part in range(CORES):
                from_core = core if part == 0 else 1 - core
                z0 = (from_chip * CORES + from_core) * tile_z
                for z in range(tile_z):
                    planes = [piece[part, k, z].astype(F32) for k in range(PARTS)]
                    now = planes[0] + planes[1]
                    one_ref[z0 + z + 1, pl.ds(y0 + 8, tile_y)] = now
                    two_ref[z0 + z + 1, pl.ds(y0 + 8, tile_y)] = now - (planes[2] + planes[3])
                    speed_ref[z0 + z, pl.ds(y0, tile_y)] = lookup(table, planes[4].astype(jnp.int32))

    lane = lax.broadcasted_iota(jnp.int32, (1, cols), 1)
    for i in range(sources):
        speed_row = speed_ref[src_pos_ref[i, 0], pl.ds(src_pos_ref[i, 1], 1)]
        row_ref[pl.ds(i, 1)] = jnp.where(lane == src_pos_ref[i, 2], speed_row, 0.0)

    lanes = lax.broadcasted_iota(jnp.int32, (8, cols), 1)
    low_side, high_side = [], []
    for j in range(1, 5):
        low_side.append(jnp.where(lanes >= j, STENCIL_WEIGHTS[j], 0.0))
        high_side.append(jnp.where(lanes < cols - j, STENCIL_WEIGHTS[j], 0.0))

    def beside(ref, z, y0, distance):
        if isinstance(y0, int):
            return ref[z + 1, pl.ds(y0 + 8 + distance, 8)]
        return ref[z + 1, pl.ds(y0, 24)][8 + distance : 16 + distance]

    def stencil_rows(now_ref, new_ref, y0):
        mids = [None] * 4 + [now_ref[z + 1, pl.ds(y0 + 8, 8)] for z in range(4)]
        for z in range(depth):
            mids.append(now_ref[z + 5, pl.ds(y0 + 8, 8)] if z + 4 < depth else None)
            mid = mids[4]
            total = (3.0 * STENCIL_WEIGHTS[0]) * mid
            for j in range(1, 5):
                pairs = beside(now_ref, z, y0, j) + beside(now_ref, z, y0, -j)
                for near in (mids[4 - j], mids[4 + j]):
                    if near is not None:
                        pairs = pairs + near
                total = total + STENCIL_WEIGHTS[j] * pairs
                total = total + low_side[j - 1] * pltpu.roll(mid, j, 1)
                total = total + high_side[j - 1] * pltpu.roll(mid, cols - j, 1)
            mids.pop(0)
            old = new_ref[z + 1, pl.ds(y0 + 8, 8)]
            new_ref[z + 1, pl.ds(y0 + 8, 8)] = (2.0 * mid - old) + speed_ref[z, pl.ds(y0, 8)] * total

    def advance(now_ref, new_ref, tick):
        tiles = rows // 8
        if tiles * depth * cols <= 64 * 128:
            for tile in range(tiles):
                stencil_rows(now_ref, new_ref, tile * 8)
        else:

            def one_tile(tile, carry):
                stencil_rows(now_ref, new_ref, pl.multiple_of(tile * 8, 8))
                return carry

            lax.fori_loop(0, tiles, one_tile, 0)

        @pl.when(is_source)
        def _():
            for i in range(sources):
                at = (src_pos_ref[i, 0] + 1, pl.ds(src_pos_ref[i, 1] + 8, 1))
                new_ref[at] = new_ref[at] + wavelet_ref[i, tick] * row_ref[pl.ds(i, 1)]

        @pl.when(jnp.logical_not(is_source))
        def _():
            new_ref[1, 8 : rows + 8] = new_ref[1, 8 : rows + 8] + speed_ref[0] * added_ref[tick]

    y_own = pl.ds(pl.multiple_of(band * tile_y, tile_y) + 8, tile_y)

    def image_time(snapshot, carry):
        refs_at = (one_ref, two_ref)
        for substep in range(SUB):
            advance(refs_at[substep % 2], refs_at[1 - substep % 2], snapshot * SUB + substep)
        for out_ref, owner in ((keep_ref, role), (send_ref, chip * CORES + (1 - core))):
            for z in range(tile_z + 2):
                out_ref[snapshot, z] = refs_at[SUB % 2][owner * tile_z + z, y_own]
        return carry

    lax.fori_loop(0, steps // SUB, image_time, 0)


def propagate(pieces, bands, chips, wavelet, src_pos, table, added):
    _, _, tile_z, tile_y, cols = pieces[0].shape
    depth, rows = chips * CORES * tile_z, bands * tile_y
    steps = wavelet.shape[1]
    snaps = jax.ShapeDtypeStruct((steps // SUB, tile_z + 2, tile_y, cols), F32)
    field = pltpu.VMEM((depth + 2, rows + 16, cols), F32)
    return pl.pallas_call(
        functools.partial(step_kernel, bands, chips, steps),
        out_shape=(snaps, snaps),
        in_specs=[SMEM_SPEC] * 2 + [VMEM_SPEC] * (2 + len(pieces)),
        out_specs=(VMEM_SPEC, VMEM_SPEC),
        scratch_shapes=[
            field,
            field,
            pltpu.VMEM((depth, rows, cols), F32),
            pltpu.VMEM((max(8, src_pos.shape[0]), cols), F32),
        ],
        name="propagate",
    )(wavelet, src_pos, table, added, *pieces)


def image_kernel(lag_ref, own_ref, other_ref, image_ref, src_ref, rec_ref):
    is_source = lax.rem(lax.axis_index("role"), CORES) == 0
    images, planes, tile_y, cols = own_ref.shape
    source = [[None] * planes for _ in range(images)]
    receiver = [[None] * planes for _ in range(images)]
    for i in range(images):
        for z in range(planes):
            own, other = own_ref[i, z], other_ref[i, z]
            source[i][z] = jnp.where(is_source, own, other)
            receiver[i][z] = jnp.where(is_source, other, own)
    for z in range(planes - 2):
        src_ref[z] = source[images - 1][z + 1]
        rec_ref[z] = receiver[images - 1][z + 1]
    lanes = lax.broadcasted_iota(jnp.int32, (tile_y, cols), 1)
    for slot in range(lag_ref.shape[0]):
        lag = lag_ref[slot]
        reach = jnp.abs(lag)
        there = lax.rem(2 * cols - 2 * lag, cols)
        back = lax.rem(cols + lag, cols)
        sums = []
        for z in range(planes):
            total = None
            for i in range(images):
                term = source[i][z] * pltpu.roll(receiver[i][z], there, 1)
                total = term if total is None else total + term
            sums.append(total)
        inside = (lanes >= reach) & (lanes < cols - reach)
        for z in range(planes - 2):
            value = (2.0 * sums[z + 1] - sums[z]) - sums[z + 2]
            image_ref[slot, z] = jnp.where(inside, pltpu.roll(value, back, 1), 0.0).astype(BF16)


def make_image(lags, own, other):
    _, planes, tile_y, cols = own.shape
    field = jax.ShapeDtypeStruct((planes - 2, tile_y, cols), F32)
    return pl.pallas_call(
        image_kernel,
        out_shape=(
            jax.ShapeDtypeStruct((lags.shape[0], planes - 2, tile_y, cols), BF16),
            field,
            field,
        ),
        in_specs=[SMEM_SPEC] + [VMEM_SPEC] * 2,
        out_specs=(VMEM_SPEC,) * 3,
        name="image",
    )(lags, own, other)


def shards(
    vel_index,
    courant,
    src_now,
    src_prev,
    rec_now,
    rec_prev,
    src_pos,
    src_wavelet,
    rec_pos,
    rec_traces,
    offset_lags,
):
    bands, roles = lax.axis_size("band"), lax.axis_size("role")
    chips = roles // CORES
    cols = src_now.shape[2]
    partner = [(i, i + 1 - 2 * (i % CORES)) for i in range(roles)]

    keep, send = pack(vel_index, src_now, src_prev, rec_now, rec_prev)
    pair = jnp.stack([keep, lax.ppermute(send, "role", partner)])
    pieces = []
    for shift in range(bands):
        moved = pair
        if shift:
            moved = lax.ppermute(pair, "band", [(i, (i + shift) % bands) for i in range(bands)])
        pieces.append(moved)
        for hop in range(1, chips):
            perm = [(i, (i + CORES * hop) % roles) for i in range(roles)]
            pieces.append(lax.ppermute(moved, "role", perm))
    added = inject(rec_pos, rec_traces, bands * src_now.shape[1], cols)
    table = jnp.pad(courant, (0, 128 - courant.shape[0]))[None]
    own, outgoing = propagate(pieces, bands, chips, src_wavelet, src_pos, table, added)
    other = lax.ppermute(outgoing, "role", partner)
    return make_image(offset_lags, own, other)


def solution(mesh):
    field = P(("survey", "role"), "band", None)
    placed = (P("role", "band", None), P()) + (field,) * 4 + (P("survey", None),) * 4 + (P(),)
    return jax.shard_map(
        shards,
        mesh=mesh,
        in_specs=placed,
        out_specs=(P("survey", "role", "band", None), field, field),
        check_vma=False,
    )
```

time: 510 us -> 44.9 us (0.09); the launches traced: 502 us -> 44.5 us
  local copies, waits for them, and re-layouts: 172 us -> 1.8 us
  starting transfers between devices: 137 us -> 10.5 us
  waiting for transfers between devices: 112 us -> 7.29 us
  other arithmetic: 78.5 us -> 0.79 us
  Pallas kernels: 0 us -> 23.4 us
    ppermute x66 -> x9, starting transfers between devices: 137 us -> 10.5 us  [the longest x3 6 us: shards(): lax.ppermute(pair, 'band', [(i, (i + shift) % bands) for i in range(bands)])]
    gather x16 -> x0, local copies, waits for them, and re-layouts: 119 us -> none  [the longest x8 60.4 us: product(): lax.dynamic_slice_in_dim(source_pad, max_lag - lag_value, col_cells, 2)]
    ppermute x66 -> x9, waiting for transfers between devices: 112 us -> 7.29 us  [the longest x4 4.69 us: shards(): pieces.append(lax.ppermute(moved, 'role', perm))]
    add x49 -> x0, other arithmetic: 46.6 us -> none  [the longest x32 42.5 us: add_level(): return summed + jnp.where(vel_index == level, courant[level], 0.0)]
    dynamic_slice x48 -> x0, local copies, waits for them, and re-layouts: 43.6 us -> none  [the longest x32 40.6 us: add_level(): return summed + jnp.where(vel_index == level, courant[level], 0.0)]
    unnamed x5 -> x0, other arithmetic: 24.9 us -> none
    pallas_call x0 -> x4, Pallas kernels: none -> 23.4 us  [the longest x1 12.2 us: propagate(): pl.pallas_call(functools.partial(step_kernel, bands, chips, steps), out_s...]
  transfers between devices with their start and end apart: 66 -> 9, of which waited for: 45 -> 6; matrix products, arithmetic and copies ran while one was open for 1% -> 1% of each run, Pallas kernels for 0% -> 12%
where the time goes in v1:
time: 44.9 us; the launch traced here: 44.5 us
  Pallas kernels  23.4 us (52%)
  starting transfers between devices  10.5 us (23%)
  waiting for transfers between devices  7.29 us (16%)
  local copies, waits for them, and re-layouts  1.8 us (4%)
  other arithmetic  0.79 us (2%)
  between operations  0.69 us (2%)
    pallas_call x1, Pallas kernels, propagate(): pl.pallas_call(functools.partial(step_kernel, bands, chips, steps), out_s...  12.2 us
    ppermute x3, starting transfers between devices, shards(): lax.ppermute(pair, 'band', [(i, (i + shift) % bands) for i in range(bands)])  6 us
    pallas_call x1, Pallas kernels, inject(): pl.pallas_call(functools.partial(inject_kernel, chunk), out_shape=jax.Sha...  5.28 us
    ppermute x4, waiting for transfers between devices, shards(): pieces.append(lax.ppermute(moved, 'role', perm))  4.69 us
    pallas_call x1, Pallas kernels, make_image(): pl.pallas_call(image_kernel, out_shape=(jax.ShapeDtypeStruct((lags.shape[...  4.54 us
    ppermute x4, starting transfers between devices, shards(): pieces.append(lax.ppermute(moved, 'role', perm))  4.05 us
    ppermute x1, waiting for transfers between devices, shards(): other = lax.ppermute(outgoing, 'role', partner)  1.51 us
    pallas_call x1, Pallas kernels, pack(): pl.pallas_call(pack_kernel, out_shape=(shape, shape), in_specs=[VMEM_SPEC...  1.42 us
  transfers between devices with their start and end apart: 9, of which 6 were waited for; matrix products, arithmetic and copies ran while one was open for 1% of the time, Pallas kernels for 12%

profile of v1, /device:TPU:0, one launch (start us, length us, event | category | flops | bytes accessed | tf_op | source)
XLA Modules:
  0.0 44.5 jit_solution(5884571102834178057)
XLA Ops:
  0.6 1.4 %pack.1 = (bf16[5,4,8,128]{3,2,1,0:T(8,128)(2,1)}, bf16[5,4,8,128]{3,2,1,0:T(8,128)(2,1)}) custom-call(s32[4,8,128]{2,1,0:T(8,128)} %vel_ref.1, f32[4,8,128]{2,1,0:T(8,128)} %sn_ref.1, f32[4,8,128]{2,1,0:T(8,128)} %sp_ref.1, f32[4,8,128]{2,1,0:T(8,128)} %rn_ref.1, f32[4,8,128]{2,1,0:T(8,128)} %rp_ref.1), custom_call_target="tpu_custom_call" | custom-call | tf_op jit(solution)/shard_map/pack/pallas_call | solution.py:43
  2.1 0.5 %collective-permute-start = (bf16[5,4,8,128]{3,2,1,0:T(8,128)(2,1)}, bf16[5,4,8,128]{3,2,1,0:T(8,128)(2,1)S(1)}, u32[]{:S(2)}, u32[]{:S(2)}) collective-permute-start(bf16[5,4,8,128]{3,2,1,0:T(8,128)(2,1)} %get-tuple-element.8), channel_id=1, source_target_pairs={{0,1},{1,0},{2,3},{3,2},{4,5},{5,4},{6,7},{7,6},{8,9},{9,8},{10,11... | collective-permute-start | bytes 122888 | tf_op jit(solution)/shard_map/ppermute | solution.py:299
  2.5 1.1 %collective-permute-done = bf16[5,4,8,128]{3,2,1,0:T(8,128)(2,1)S(1)} collective-permute-done((bf16[5,4,8,128]{3,2,1,0:T(8,128)(2,1)}, bf16[5,4,8,128]{3,2,1,0:T(8,128)(2,1)S(1)}, u32[]{:S(2)}, u32[]{:S(2)}) %collective-permute-start) | collective-permute-done | bytes 40992 | tf_op jit(solution)/shard_map/ppermute | solution.py:299
  3.6 0.8 %pad_maximum_fusion.refs_4_ = bf16[2,5,4,8,128]{4,3,2,1,0:T(8,128)(2,1)S(1)} fusion(bf16[1,5,4,8,128]{4,3,2,1,0:T(8,128)(2,1)S(1)} %bitcast.8, bf16[1,5,4,8,128]{4,3,2,1,0:T(8,128)(2,1)} %bitcast.7), kind=kLoop, calls=%fused_computation | loop fusion | flops 40960 | bytes 163840 | tf_op jit(solution)/shard_map/stack | solution.py:299
  4.4 5.0 %collective-permute-start.6 = (bf16[2,5,4,8,128]{4,3,2,1,0:T(8,128)(2,1)S(1)}, bf16[2,5,4,8,128]{4,3,2,1,0:T(8,128)(2,1)S(1)}, u32[]{:S(2)}, u32[]{:S(2)}) collective-permute-start(bf16[2,5,4,8,128]{4,3,2,1,0:T(8,128)(2,1)S(1)} %pad_maximum_fusion.refs_4_), channel_id=1, source_target_pairs={{0,12},{4,0},{8,4},{12,8},{1,13},{5,1},{9,5},{13,9},{2,14},{6,2},{... | collective-permute-start | bytes 245768 | tf_op jit(solution)/shard_map/ppermute | solution.py:304
  9.4 1.0 %collective-permute-start.2 = (bf16[2,5,4,8,128]{4,3,2,1,0:T(8,128)(2,1)S(1)}, bf16[2,5,4,8,128]{4,3,2,1,0:T(8,128)(2,1)S(1)}, u32[]{:S(2)}, u32[]{:S(2)}) collective-permute-start(bf16[2,5,4,8,128]{4,3,2,1,0:T(8,128)(2,1)S(1)} %pad_maximum_fusion.refs_4_), channel_id=1, source_target_pairs={{0,4},{4,8},{8,12},{12,0},{1,5},{5,9},{9,13},{13,1},{2,6},{6,10},{... | collective-permute-start | bytes 245768 | tf_op jit(solution)/shard_map/ppermute | solution.py:304
  10.4 5.3 %inject.1.refs_3_ = f32[16,32,128]{2,1,0:T(8,128)} custom-call(s32[2,4096]{1,0:T(2,128)} %bitcast.9, f32[16,4096]{1,0:T(8,128)} %bitcast.6), custom_call_target="tpu_custom_call" | custom-call | tf_op jit(solution)/shard_map/inject/pallas_call | solution.py:85
  15.7 1.5 %collective-permute-start.1 = (bf16[2,5,4,8,128]{4,3,2,1,0:T(8,128)(2,1)S(1)}, bf16[2,5,4,8,128]{4,3,2,1,0:T(8,128)(2,1)S(1)}, u32[]{:S(2)}, u32[]{:S(2)}) collective-permute-start(bf16[2,5,4,8,128]{4,3,2,1,0:T(8,128)(2,1)S(1)} %pad_maximum_fusion.refs_4_), channel_id=1, source_target_pairs={{0,2},{1,3},{2,0},{3,1},{4,6},{5,7},{6,4},{7,5},{8,10},{9,11},{10,... | collective-permute-start | bytes 245768 | tf_op jit(solution)/shard_map/ppermute | solution.py:308
  17.2 0.0 collective-permute-done.6.refs_10_
  17.2 0.5 %collective-permute-start.7 = (bf16[2,5,4,8,128]{4,3,2,1,0:T(8,128)(2,1)S(1)}, bf16[2,5,4,8,128]{4,3,2,1,0:T(8,128)(2,1)S(1)}, u32[]{:S(2)}, u32[]{:S(2)}) collective-permute-start(bf16[2,5,4,8,128]{4,3,2,1,0:T(8,128)(2,1)S(1)} %collective-permute-done.6.refs_10_), channel_id=1, source_target_pairs={{0,2},{1,3},{2,0},{3,1},{4,6},{5,7},{6,4},{7,5},{8,10},{9,11},{10,... | collective-permute-start | bytes 245768 | tf_op jit(solution)/shard_map/ppermute | solution.py:308
  17.7 0.0 collective-permute-done.4.refs_8_
  17.7 1.5 %collective-permute-start.5 = (bf16[2,5,4,8,128]{4,3,2,1,0:T(8,128)(2,1)S(1)}, bf16[2,5,4,8,128]{4,3,2,1,0:T(8,128)(2,1)S(1)}, u32[]{:S(2)}, u32[]{:S(2)}) collective-permute-start(bf16[2,5,4,8,128]{4,3,2,1,0:T(8,128)(2,1)S(1)} %collective-permute-done.4.refs_8_), channel_id=1, source_target_pairs={{0,2},{1,3},{2,0},{3,1},{4,6},{5,7},{6,4},{7,5},{8,10},{9,11},{10,... | collective-permute-start | bytes 245768 | tf_op jit(solution)/shard_map/ppermute | solution.py:308
  19.2 0.0 collective-permute-done.2.refs_6_
  19.3 0.5 %collective-permute-start.3 = (bf16[2,5,4,8,128]{4,3,2,1,0:T(8,128)(2,1)S(1)}, bf16[2,5,4,8,128]{4,3,2,1,0:T(8,128)(2,1)S(1)}, u32[]{:S(2)}, u32[]{:S(2)}) collective-permute-start(bf16[2,5,4,8,128]{4,3,2,1,0:T(8,128)(2,1)S(1)} %collective-permute-done.2.refs_6_), channel_id=1, source_target_pairs={{0,2},{1,3},{2,0},{3,1},{4,6},{5,7},{6,4},{7,5},{8,10},{9,11},{10,... | collective-permute-start | bytes 245768 | tf_op jit(solution)/shard_map/ppermute | solution.py:308
  19.8 0.5 %pad_bitcast_fusion.refs_2_ = f32[1,128]{1,0:T(1,128)} fusion(f32[32]{0:T(128)S(1)} %copy-done.9), kind=kLoop, calls=%fused_computation.1 | loop fusion | bytes 640 | tf_op jit(solution)/shard_map/broadcast_in_dim | solution.py:310
  20.3 0.7 %collective-permute-done.1.refs_5_ = bf16[2,5,4,8,128]{4,3,2,1,0:T(8,128)(2,1)S(1)} collective-permute-done((bf16[2,5,4,8,128]{4,3,2,1,0:T(8,128)(2,1)S(1)}, bf16[2,5,4,8,128]{4,3,2,1,0:T(8,128)(2,1)S(1)}, u32[]{:S(2)}, u32[]{:S(2)}) %collective-permute-start.1) | collective-permute-done | bytes 81952 | tf_op jit(solution)/shard_map/ppermute | solution.py:308
  21.0 1.8 %collective-permute-done.7.refs_11_ = bf16[2,5,4,8,128]{4,3,2,1,0:T(8,128)(2,1)S(1)} collective-permute-done((bf16[2,5,4,8,128]{4,3,2,1,0:T(8,128)(2,1)S(1)}, bf16[2,5,4,8,128]{4,3,2,1,0:T(8,128)(2,1)S(1)}, u32[]{:S(2)}, u32[]{:S(2)}) %collective-permute-start.7) | collective-permute-done | bytes 81952 | tf_op jit(solution)/shard_map/ppermute | solution.py:308
  22.8 1.3 %collective-permute-done.5.refs_9_ = bf16[2,5,4,8,128]{4,3,2,1,0:T(8,128)(2,1)S(1)} collective-permute-done((bf16[2,5,4,8,128]{4,3,2,1,0:T(8,128)(2,1)S(1)}, bf16[2,5,4,8,128]{4,3,2,1,0:T(8,128)(2,1)S(1)}, u32[]{:S(2)}, u32[]{:S(2)}) %collective-permute-start.5) | collective-permute-done | bytes 81952 | tf_op jit(solution)/shard_map/ppermute | solution.py:308
  24.1 0.9 %collective-permute-done.3.refs_7_ = bf16[2,5,4,8,128]{4,3,2,1,0:T(8,128)(2,1)S(1)} collective-permute-done((bf16[2,5,4,8,128]{4,3,2,1,0:T(8,128)(2,1)S(1)}, bf16[2,5,4,8,128]{4,3,2,1,0:T(8,128)(2,1)S(1)}, u32[]{:S(2)}, u32[]{:S(2)}) %collective-permute-start.3) | collective-permute-done | bytes 81952 | tf_op jit(solution)/shard_map/ppermute | solution.py:308
  25.0 0.6 %copy-done.8 = bf16[2,5,4,8,128]{4,3,2,1,0:T(8,128)(2,1)} copy-done((bf16[2,5,4,8,128]{4,3,2,1,0:T(8,128)(2,1)}, bf16[2,5,4,8,128]{4,3,2,1,0:T(8,128)(2,1)S(1)}, u32[]{:S(2)}) %copy-start.8) | copy-done | bytes 81944
  25.7 12.2 %propagate.1 = (f32[4,6,8,128]{3,2,1,0:T(8,128)}, f32[4,6,8,128]{3,2,1,0:T(8,128)}) custom-call(f32[4,16]{1,0:T(4,128)} %refs_0_.1, s32[4,3]{1,0:T(4,128)} %refs_1_.1, f32[1,128]{1,0:T(1,128)} %pad_bitcast_fusion.refs_2_, f32[16,32,128]{2,1,0:T(8,128)} %inject.1.refs_3_, bf16[2,5,4,8,128]{4,3,2,1,0:T(8,128)(2,1)} %copy-done, ...), custom_call_target="tpu_custom_call" | custom-call | tf_op jit(solution)/shard_map/propagate/pallas_call | solution.py:217
  37.8 1.5 %collective-permute-done.8.other_ref = f32[4,6,8,128]{3,2,1,0:T(8,128)S(1)} collective-permute-done((f32[4,6,8,128]{3,2,1,0:T(8,128)}, f32[4,6,8,128]{3,2,1,0:T(8,128)S(1)}, u32[]{:S(2)}, u32[]{:S(2)}) %collective-permute-start.8) | collective-permute-done | bytes 98336 | tf_op jit(solution)/shard_map/ppermute | solution.py:312
  39.3 0.6 %copy-done.1 = f32[4,6,8,128]{3,2,1,0:T(8,128)} copy-done((f32[4,6,8,128]{3,2,1,0:T(8,128)}, f32[4,6,8,128]{3,2,1,0:T(8,128)S(1)}, u32[]{:S(2)}) %copy-start.1) | copy-done | bytes 98328
  40.0 4.5 %image.1 = (bf16[32,4,8,128]{3,2,1,0:T(8,128)(2,1)}, f32[4,8,128]{2,1,0:T(8,128)}, f32[4,8,128]{2,1,0:T(8,128)}) custom-call(s32[32]{0:T(128)} %lag_ref.1, f32[4,6,8,128]{3,2,1,0:T(8,128)} %get-tuple-element.9.own_ref, f32[4,6,8,128]{3,2,1,0:T(8,128)} %copy-done.1), custom_call_target="tpu_custom_call" | custom-call | tf_op jit(solution)/shard_map/image/pallas_call | solution.py:267
  (20 shorter events, 0.0 us)
Async XLA Ops:
  2.1 1.6 %collective-permute-start = (bf16[5,4,8,128]{3,2,1,0:T(8,128)(2,1)}, bf16[5,4,8,128]{3,2,1,0:T(8,128)(2,1)S(1)}, u32[]{:S(2)}, u32[]{:S(2)}) collective-permute-start(bf16[5,4,8,128]{3,2,1,0:T(8,128)(2,1)} %get-tuple-element.8), channel_id=1, source_target_pairs={{0,1},{1,0},{2,3},{3,2},{4,5},{5,4},{6,7},{7,6},{8,9},{9,8},{10,11... | collective-permute-start | bytes 122888 | tf_op jit(solution)/shard_map/ppermute | solution.py:299
  4.4 11.3 %copy-start = (bf16[2,5,4,8,128]{4,3,2,1,0:T(8,128)(2,1)}, bf16[2,5,4,8,128]{4,3,2,1,0:T(8,128)(2,1)S(1)}, u32[]{:S(2)}) copy-start(bf16[2,5,4,8,128]{4,3,2,1,0:T(8,128)(2,1)S(1)} %pad_maximum_fusion.refs_4_) | copy-start | bytes 245764
  4.4 12.8 %collective-permute-start.6 = (bf16[2,5,4,8,128]{4,3,2,1,0:T(8,128)(2,1)S(1)}, bf16[2,5,4,8,128]{4,3,2,1,0:T(8,128)(2,1)S(1)}, u32[]{:S(2)}, u32[]{:S(2)}) collective-permute-start(bf16[2,5,4,8,128]{4,3,2,1,0:T(8,128)(2,1)S(1)} %pad_maximum_fusion.refs_4_), channel_id=1, source_target_pairs={{0,12},{4,0},{8,4},{12,8},{1,13},{5,1},{9,5},{13,9},{2,14},{6,2},{... | collective-permute-start | bytes 245768 | tf_op jit(solution)/shard_map/ppermute | solution.py:304
  9.4 8.3 %collective-permute-start.4 = (bf16[2,5,4,8,128]{4,3,2,1,0:T(8,128)(2,1)S(1)}, bf16[2,5,4,8,128]{4,3,2,1,0:T(8,128)(2,1)S(1)}, u32[]{:S(2)}, u32[]{:S(2)}) collective-permute-start(bf16[2,5,4,8,128]{4,3,2,1,0:T(8,128)(2,1)S(1)} %pad_maximum_fusion.refs_4_), channel_id=1, source_target_pairs={{0,8},{4,12},{8,0},{12,4},{1,9},{5,13},{9,1},{13,5},{2,10},{6,14},... | collective-permute-start | bytes 245768 | tf_op jit(solution)/shard_map/ppermute | solution.py:304
  9.4 9.8 %collective-permute-start.2 = (bf16[2,5,4,8,128]{4,3,2,1,0:T(8,128)(2,1)S(1)}, bf16[2,5,4,8,128]{4,3,2,1,0:T(8,128)(2,1)S(1)}, u32[]{:S(2)}, u32[]{:S(2)}) collective-permute-start(bf16[2,5,4,8,128]{4,3,2,1,0:T(8,128)(2,1)S(1)} %pad_maximum_fusion.refs_4_), channel_id=1, source_target_pairs={{0,4},{4,8},{8,12},{12,0},{1,5},{5,9},{9,13},{13,1},{2,6},{6,10},{... | collective-permute-start | bytes 245768 | tf_op jit(solution)/shard_map/ppermute | solution.py:304
  10.4 9.4 %copy-start.9 = (f32[32]{0:T(128)S(1)}, f32[32]{0:T(128)}, u32[]{:S(2)}) copy-start(f32[32]{0:T(128)} %param.12) | copy-start | bytes 388
  15.7 5.3 %collective-permute-start.1 = (bf16[2,5,4,8,128]{4,3,2,1,0:T(8,128)(2,1)S(1)}, bf16[2,5,4,8,128]{4,3,2,1,0:T(8,128)(2,1)S(1)}, u32[]{:S(2)}, u32[]{:S(2)}) collective-permute-start(bf16[2,5,4,8,128]{4,3,2,1,0:T(8,128)(2,1)S(1)} %pad_maximum_fusion.refs_4_), channel_id=1, source_target_pairs={{0,2},{1,3},{2,0},{3,1},{4,6},{5,7},{6,4},{7,5},{8,10},{9,11},{10,... | collective-permute-start | bytes 245768 | tf_op jit(solution)/shard_map/ppermute | solution.py:308
  17.2 7.8 %copy-start.2 = (bf16[2,5,4,8,128]{4,3,2,1,0:T(8,128)(2,1)}, bf16[2,5,4,8,128]{4,3,2,1,0:T(8,128)(2,1)S(1)}, u32[]{:S(2)}) copy-start(bf16[2,5,4,8,128]{4,3,2,1,0:T(8,128)(2,1)S(1)} %collective-permute-done.6.refs_10_) | copy-start | bytes 245764
  17.2 5.6 %collective-permute-start.7 = (bf16[2,5,4,8,128]{4,3,2,1,0:T(8,128)(2,1)S(1)}, bf16[2,5,4,8,128]{4,3,2,1,0:T(8,128)(2,1)S(1)}, u32[]{:S(2)}, u32[]{:S(2)}) collective-permute-start(bf16[2,5,4,8,128]{4,3,2,1,0:T(8,128)(2,1)S(1)} %collective-permute-done.6.refs_10_), channel_id=1, source_target_pairs={{0,2},{1,3},{2,0},{3,1},{4,6},{5,7},{6,4},{7,5},{8,10},{9,11},{10,... | collective-permute-start | bytes 245768 | tf_op jit(solution)/shard_map/ppermute | solution.py:308
  17.7 7.3 %copy-start.3 = (bf16[2,5,4,8,128]{4,3,2,1,0:T(8,128)(2,1)}, bf16[2,5,4,8,128]{4,3,2,1,0:T(8,128)(2,1)S(1)}, u32[]{:S(2)}) copy-start(bf16[2,5,4,8,128]{4,3,2,1,0:T(8,128)(2,1)S(1)} %collective-permute-done.4.refs_8_) | copy-start | bytes 245764
  17.7 6.4 %collective-permute-start.5 = (bf16[2,5,4,8,128]{4,3,2,1,0:T(8,128)(2,1)S(1)}, bf16[2,5,4,8,128]{4,3,2,1,0:T(8,128)(2,1)S(1)}, u32[]{:S(2)}, u32[]{:S(2)}) collective-permute-start(bf16[2,5,4,8,128]{4,3,2,1,0:T(8,128)(2,1)S(1)} %collective-permute-done.4.refs_8_), channel_id=1, source_target_pairs={{0,2},{1,3},{2,0},{3,1},{4,6},{5,7},{6,4},{7,5},{8,10},{9,11},{10,... | collective-permute-start | bytes 245768 | tf_op jit(solution)/shard_map/ppermute | solution.py:308
  19.3 5.8 %copy-start.4 = (bf16[2,5,4,8,128]{4,3,2,1,0:T(8,128)(2,1)}, bf16[2,5,4,8,128]{4,3,2,1,0:T(8,128)(2,1)S(1)}, u32[]{:S(2)}) copy-start(bf16[2,5,4,8,128]{4,3,2,1,0:T(8,128)(2,1)S(1)} %collective-permute-done.2.refs_6_) | copy-start | bytes 245764
  19.3 5.7 %collective-permute-start.3 = (bf16[2,5,4,8,128]{4,3,2,1,0:T(8,128)(2,1)S(1)}, bf16[2,5,4,8,128]{4,3,2,1,0:T(8,128)(2,1)S(1)}, u32[]{:S(2)}, u32[]{:S(2)}) collective-permute-start(bf16[2,5,4,8,128]{4,3,2,1,0:T(8,128)(2,1)S(1)} %collective-permute-done.2.refs_6_), channel_id=1, source_target_pairs={{0,2},{1,3},{2,0},{3,1},{4,6},{5,7},{6,4},{7,5},{8,10},{9,11},{10,... | collective-permute-start | bytes 245768 | tf_op jit(solution)/shard_map/ppermute | solution.py:308
  21.0 4.0 %copy-start.5 = (bf16[2,5,4,8,128]{4,3,2,1,0:T(8,128)(2,1)}, bf16[2,5,4,8,128]{4,3,2,1,0:T(8,128)(2,1)S(1)}, u32[]{:S(2)}) copy-start(bf16[2,5,4,8,128]{4,3,2,1,0:T(8,128)(2,1)S(1)} %collective-permute-done.1.refs_5_) | copy-start | bytes 245764
  22.8 2.2 %copy-start.6 = (bf16[2,5,4,8,128]{4,3,2,1,0:T(8,128)(2,1)}, bf16[2,5,4,8,128]{4,3,2,1,0:T(8,128)(2,1)S(1)}, u32[]{:S(2)}) copy-start(bf16[2,5,4,8,128]{4,3,2,1,0:T(8,128)(2,1)S(1)} %collective-permute-done.7.refs_11_) | copy-start | bytes 245764
  24.1 0.9 %copy-start.7 = (bf16[2,5,4,8,128]{4,3,2,1,0:T(8,128)(2,1)}, bf16[2,5,4,8,128]{4,3,2,1,0:T(8,128)(2,1)S(1)}, u32[]{:S(2)}) copy-start(bf16[2,5,4,8,128]{4,3,2,1,0:T(8,128)(2,1)S(1)} %collective-permute-done.5.refs_9_) | copy-start | bytes 245764
  25.0 0.6 %copy-start.8 = (bf16[2,5,4,8,128]{4,3,2,1,0:T(8,128)(2,1)}, bf16[2,5,4,8,128]{4,3,2,1,0:T(8,128)(2,1)S(1)}, u32[]{:S(2)}) copy-start(bf16[2,5,4,8,128]{4,3,2,1,0:T(8,128)(2,1)S(1)} %collective-permute-done.3.refs_7_) | copy-start | bytes 245764
  37.8 1.5 %collective-permute-start.8 = (f32[4,6,8,128]{3,2,1,0:T(8,128)}, f32[4,6,8,128]{3,2,1,0:T(8,128)S(1)}, u32[]{:S(2)}, u32[]{:S(2)}) collective-permute-start(f32[4,6,8,128]{3,2,1,0:T(8,128)} %get-tuple-element.10), channel_id=1, source_target_pairs={{0,1},{1,0},{2,3},{3,2},{4,5},{5,4},{6,7},{7,6},{8,9},{9,8},{10,11... | collective-permute-start | bytes 294920 | tf_op jit(solution)/shard_map/ppermute | solution.py:312
  39.3 0.6 %copy-start.1 = (f32[4,6,8,128]{3,2,1,0:T(8,128)}, f32[4,6,8,128]{3,2,1,0:T(8,128)S(1)}, u32[]{:S(2)}) copy-start(f32[4,6,8,128]{3,2,1,0:T(8,128)S(1)} %collective-permute-done.8.other_ref) | copy-start | bytes 294916

commit v2 on v1

v2 whole, which is shorter than its diff:
```python
import functools

import jax
import jax.numpy as jnp
from jax import lax
from jax.experimental import pallas as pl
from jax.experimental.pallas import tpu as pltpu
from jax.sharding import PartitionSpec as P

SUB = 4
IMAGES = 4
PARTS = 5
CORES = 2

STENCIL_WEIGHTS = (-205.0 / 72.0, 8.0 / 5.0, -1.0 / 5.0, 8.0 / 315.0, -1.0 / 560.0)
F32 = jnp.float32
BF16 = jnp.bfloat16

VMEM_SPEC = pl.BlockSpec(memory_space=pltpu.VMEM)
SMEM_SPEC = pl.BlockSpec(memory_space=pltpu.SMEM)
ANY_SPEC = pl.BlockSpec(memory_space=pl.ANY)


def on_chip(value):
    return pltpu.with_memory_space_constraint(value, pltpu.VMEM)


def params(scratch_bytes):
    return pltpu.CompilerParams(vmem_limit_bytes=scratch_bytes + scratch_bytes // 4 + (4 << 20))


def split(value):
    high = value.astype(BF16)
    return high, (value - high.astype(F32)).astype(BF16)


def pack_kernel(vel_ref, sn_ref, sp_ref, rn_ref, rp_ref, pair_ref, send_ref):
    core = lax.rem(lax.axis_index("role"), CORES)
    entry = vel_ref[...].astype(F32).astype(BF16)
    src_now, rec_now = sn_ref[...], rn_ref[...]
    src_step, rec_step = src_now - sp_ref[...], rec_now - rp_ref[...]
    for out_ref, wants_source in ((pair_ref.at[0], core == 0), (send_ref, core != 0)):
        now = jnp.where(wants_source, src_now, rec_now)
        step = jnp.where(wants_source, src_step, rec_step)
        out_ref[0], out_ref[1] = split(now)
        out_ref[2], out_ref[3] = split(step)
        out_ref[4] = entry


def pack(vel_index, src_now, src_prev, rec_now, rec_prev):
    shape = (PARTS,) + src_now.shape
    return pl.pallas_call(
        pack_kernel,
        out_shape=(pltpu.VMEM((CORES,) + shape, BF16), pltpu.VMEM(shape, BF16)),
        in_specs=[VMEM_SPEC] * 5,
        out_specs=(VMEM_SPEC, VMEM_SPEC),
        compiler_params=params(0),
        name="pack",
    )(vel_index, src_now, src_prev, rec_now, rec_prev)


def inject_kernel(chunk, pos_ref, amp_ref, out_ref, acc_ref):
    count = amp_ref.shape[1]
    steps, rows, cols = out_ref.shape
    own = pl.ds(pl.multiple_of(lax.rem(lax.axis_index("role"), CORES) * steps, steps), steps)
    acc_ref[...] = jnp.zeros_like(acc_ref)

    def one(at, carry):
        span = pl.ds(pl.multiple_of(at * chunk, chunk), chunk)
        pos = pos_ref[:, span]
        in_row = lax.broadcasted_iota(jnp.int32, (rows, chunk), 0) == pos[0:1]
        in_col = lax.broadcasted_iota(jnp.int32, (cols, chunk), 0) == pos[1:2]
        col_hot = jnp.where(in_col, 1.0, 0.0).astype(BF16)
        amp = amp_ref[own, span]
        high = amp.astype(BF16).astype(F32)
        total = None
        for part in (high, amp - high):
            spread = jnp.concatenate(
                [jnp.where(in_row, part[k : k + 1], 0.0).astype(BF16) for k in range(steps)], axis=0
            )
            added = lax.dot_general(
                spread, col_hot, (((1,), (1,)), ((), ())), preferred_element_type=F32
            )
            total = added if total is None else total + added
        acc_ref[...] += total
        return carry

    lax.fori_loop(0, count // chunk, one, 0)
    for k in range(steps):
        out_ref[k] = acc_ref[k * rows : (k + 1) * rows]


def inject(rec_pos, rec_traces, rows, cols):
    count, steps = rec_traces.shape
    own_steps = steps // CORES
    chunk = next(c for c in (512, 256, 128, count) if count % c == 0)
    scratch = own_steps * rows * cols * 4
    return pl.pallas_call(
        functools.partial(inject_kernel, chunk),
        out_shape=pltpu.VMEM((own_steps, rows, cols), F32),
        in_specs=[VMEM_SPEC] * 2,
        out_specs=VMEM_SPEC,
        scratch_shapes=[pltpu.VMEM((own_steps * rows, cols), F32)],
        compiler_params=params(6 * scratch),
        name="inject",
    )(on_chip(rec_pos.T), on_chip(rec_traces.T))


def lookup(table, entry):
    width = table.shape[1]
    pieces = [
        jnp.take_along_axis(table, entry[:, at : at + width], axis=1)
        for at in range(0, entry.shape[1], width)
    ]
    return pieces[0] if len(pieces) == 1 else jnp.concatenate(pieces, axis=1)


def shift_weights(cols):
    apart = lax.broadcasted_iota(jnp.int32, (cols, cols), 0)
    apart = jnp.abs(apart - lax.broadcasted_iota(jnp.int32, (cols, cols), 1))
    weights = jnp.zeros((cols, cols), F32)
    for j in range(1, 5):
        weights = jnp.where(apart == j, STENCIL_WEIGHTS[j], weights)
    return split(weights)


def step_kernel(bands, chips, steps, *refs):
    wavelet_ref, src_pos_ref, courant_ref, late_ref, early_ref = refs[:5]
    piece_refs = refs[5 : 5 + bands * chips]
    keep_ref, send_ref = refs[5 + bands * chips : 7 + bands * chips]
    one_ref, two_ref, speed_ref, row_ref, table_ref, mix_ref, one_split, two_split = refs[
        7 + bands * chips :
    ]
    _, _, tile_z, tile_y, cols = piece_refs[0].shape
    depth, rows, _ = speed_ref.shape
    role, band = lax.axis_index("role"), lax.axis_index("band")
    core, chip = lax.rem(role, CORES), lax.div(role, CORES)
    is_source = core == 0
    sources = src_pos_ref.shape[0]
    tiles = rows // 8
    unroll = tiles * depth * cols <= 64 * 128

    for ref in (one_ref, two_ref):
        edge = jnp.zeros((rows + 16, cols), F32)
        ref[0] = edge
        ref[depth + 1] = edge
        for z in range(1, depth + 1):
            ref[z, 0:8] = edge[0:8]
            ref[z, rows + 8 :] = edge[0:8]

    high, low = shift_weights(cols)
    for at in (0, cols):
        mix_ref[at : at + cols, 0:cols] = high
        mix_ref[at : at + cols, cols:] = low

    table_ref[...] = jnp.zeros_like(table_ref)
    table_ref[:, 0 : courant_ref.shape[1]] = jnp.broadcast_to(
        courant_ref[...], (table_ref.shape[0], courant_ref.shape[1])
    )
    table = table_ref[...]
    for shift in range(bands):
        from_band = lax.rem(band + (bands - shift), bands)
        y0 = pl.multiple_of(from_band * tile_y, tile_y)
        for hop in range(chips):
            from_chip = lax.rem(chip + (chips - hop), chips)
            piece = piece_refs[shift * chips + hop]
            for part in range(CORES):
                from_core = core if part == 0 else 1 - core
                z0 = (from_chip * CORES + from_core) * tile_z
                for z in range(tile_z):
                    planes = [piece[part, k, z].astype(F32) for k in range(PARTS)]
                    now = planes[0] + planes[1]
                    one_ref[z0 + z + 1, pl.ds(y0 + 8, tile_y)] = now
                    two_ref[z0 + z + 1, pl.ds(y0 + 8, tile_y)] = now - (planes[2] + planes[3])
                    speed_ref[z0 + z, pl.ds(y0, tile_y)] = lookup(table, planes[4].astype(jnp.int32))

    lane = lax.broadcasted_iota(jnp.int32, (1, cols), 1)
    for i in range(sources):
        speed_row = speed_ref[src_pos_ref[i, 0], pl.ds(src_pos_ref[i, 1], 1)]
        row_ref[pl.ds(i, 1)] = jnp.where(lane == src_pos_ref[i, 2], speed_row, 0.0)

    def over_tiles(do):
        if unroll:
            for tile in range(tiles):
                do(tile * 8)
        else:

            def one_tile(tile, carry):
                do(pl.multiple_of(tile * 8, 8))
                return carry

            lax.fori_loop(0, tiles, one_tile, 0)

    def rows_of(y0, count):
        return pl.ds(y0 * depth if unroll else pl.multiple_of(y0 * depth, 8 * depth), count)

    def store_split(split_ref, y0, z, two_planes):
        high, low = split(two_planes)
        start = y0 * depth + z * 8
        at = pl.ds(start if unroll else pl.multiple_of(start, 16), 16)
        split_ref[at, 0:cols] = high
        split_ref[at, cols:] = low

    def beside(ref, z, y0, distance):
        if unroll:
            return ref[z + 1, pl.ds(y0 + 8 + distance, 8)]
        return ref[z + 1, pl.ds(y0, 24)][8 + distance : 16 + distance]

    def first_split(y0):
        for z in range(0, depth, 2):
            planes = [one_ref[z + k + 1, pl.ds(y0 + 8, 8)] for k in range(2)]
            store_split(one_split, y0, z, jnp.concatenate(planes, axis=0))

    over_tiles(first_split)

    def advance(now_ref, now_split, new_ref, new_split, tick):
        @pl.when(is_source)
        def _():
            for i in range(sources):
                at = (src_pos_ref[i, 0] + 1, pl.ds(src_pos_ref[i, 1] + 8, 1))
                new_ref[at] = new_ref[at] - wavelet_ref[i, tick] * row_ref[pl.ds(i, 1)]

        @pl.when(jnp.logical_not(is_source))
        def _():
            half = late_ref.shape[0]
            at = lax.rem(tick, half)
            added = jnp.where(tick < half, early_ref[at], late_ref[at])
            new_ref[1, 8 : rows + 8] = new_ref[1, 8 : rows + 8] - speed_ref[0] * added

        def stencil(y0):
            inline = lax.dot_general(
                now_split[rows_of(y0, 8 * depth)],
                mix_ref[...],
                (((1,), (0,)), ((), ())),
                preferred_element_type=F32,
            )
            inline = inline[:, 0:cols] + inline[:, cols:]
            mids = [None] * 4 + [now_ref[z + 1, pl.ds(y0 + 8, 8)] for z in range(4)]
            planes = []
            for z in range(depth):
                mids.append(now_ref[z + 5, pl.ds(y0 + 8, 8)] if z + 4 < depth else None)
                mid = mids[4]
                total = (3.0 * STENCIL_WEIGHTS[0]) * mid + inline[z * 8 : z * 8 + 8]
                for j in range(1, 5):
                    pairs = beside(now_ref, z, y0, j) + beside(now_ref, z, y0, -j)
                    for near in (mids[4 - j], mids[4 + j]):
                        if near is not None:
                            pairs = pairs + near
                    total = total + STENCIL_WEIGHTS[j] * pairs
                mids.pop(0)
                old = new_ref[z + 1, pl.ds(y0 + 8, 8)]
                new = (2.0 * mid - old) + speed_ref[z, pl.ds(y0, 8)] * total
                new_ref[z + 1, pl.ds(y0 + 8, 8)] = new
                planes.append(new)
                if len(planes) == 2:
                    store_split(new_split, y0, z - 1, jnp.concatenate(planes, axis=0))
                    planes = []

        over_tiles(stencil)

    y_own = pl.ds(pl.multiple_of(band * tile_y, tile_y) + 8, tile_y)

    def image_time(snapshot, carry):
        fields = ((one_ref, one_split), (two_ref, two_split))
        for substep in range(SUB):
            now, new = fields[substep % 2], fields[1 - substep % 2]
            advance(*now, *new, snapshot * SUB + substep)
        for out_ref, owner in ((keep_ref, role), (send_ref, chip * CORES + (1 - core))):
            for z in range(tile_z + 2):
                out_ref[snapshot, z] = fields[SUB % 2][0][owner * tile_z + z, y_own]
        return carry

    lax.fori_loop(0, steps // SUB, image_time, 0)


def propagate(pieces, bands, chips, wavelet, src_pos, courant, late, early):
    _, _, tile_z, tile_y, cols = pieces[0].shape
    depth, rows = chips * CORES * tile_z, bands * tile_y
    steps = wavelet.shape[1]
    snaps = pltpu.VMEM((steps // SUB, tile_z + 2, tile_y, cols), F32)
    field = pltpu.VMEM((depth + 2, rows + 16, cols), F32)
    parted = pltpu.VMEM((depth * rows, 2 * cols), BF16)
    scratch = 4 * cols * (2 * (depth + 2) * (rows + 16) + 3 * depth * rows + 4 * cols)
    return pl.pallas_call(
        functools.partial(step_kernel, bands, chips, steps),
        out_shape=(snaps, snaps),
        in_specs=[SMEM_SPEC] * 2 + [VMEM_SPEC] * (3 + len(pieces)),
        out_specs=(VMEM_SPEC, VMEM_SPEC),
        scratch_shapes=[
            field,
            field,
            pltpu.VMEM((depth, rows, cols), F32),
            pltpu.VMEM((max(8, src_pos.shape[0]), cols), F32),
            pltpu.VMEM((tile_y, 128), F32),
            pltpu.VMEM((2 * cols, 2 * cols), BF16),
            parted,
            parted,
        ],
        compiler_params=params(scratch),
        name="propagate",
    )(wavelet, src_pos, courant, *map(on_chip, (late, early, *pieces)))


def image_kernel(group, lag_ref, own_ref, other_ref, image_ref, src_ref, rec_ref, *scratch):
    fields_ref, sums_ref, image_sems, field_sems = scratch
    is_source = lax.rem(lax.axis_index("role"), CORES) == 0
    images, planes, tile_y, cols = own_ref.shape
    for i in range(images):
        for z in range(planes):
            own, other = own_ref[i, z], other_ref[i, z]
            fields_ref[0, i, z] = jnp.where(is_source, own, other)
            fields_ref[1, i, z] = jnp.where(is_source, other, own)
    copies = []
    for k, out_ref in enumerate((src_ref, rec_ref)):
        copies.append(
            pltpu.make_async_copy(
                fields_ref.at[k, images - 1, pl.ds(1, planes - 2)], out_ref, field_sems.at[k]
            )
        )
        copies[-1].start()
    lanes = lax.broadcasted_iota(jnp.int32, (tile_y, cols), 1)
    for slot in range(lag_ref.shape[0]):
        lag = lag_ref[slot]
        reach = jnp.abs(lag)
        there = lax.rem(2 * cols - 2 * lag, cols)
        back = lax.rem(cols + lag, cols)
        sums = []
        for z in range(planes):
            total = None
            for i in range(images):
                term = fields_ref[0, i, z] * pltpu.roll(fields_ref[1, i, z], there, 1)
                total = term if total is None else total + term
            sums.append(total)
        inside = (lanes >= reach) & (lanes < cols - reach)
        for z in range(planes - 2):
            value = (2.0 * sums[z + 1] - sums[z]) - sums[z + 2]
            sums_ref[slot, z] = jnp.where(inside, pltpu.roll(value, back, 1), 0.0).astype(BF16)
        if (slot + 1) % group == 0:
            at = pl.ds(slot + 1 - group, group)
            copies.append(
                pltpu.make_async_copy(
                    sums_ref.at[at], image_ref.at[at], image_sems.at[slot // group]
                )
            )
            copies[-1].start()
    for copy in copies:
        copy.wait()


def make_image(lags, own, other):
    images, planes, tile_y, cols = own.shape
    count = lags.shape[0]
    group = next(g for g in (8, 4, 2, 1) if count % g == 0)
    field = jax.ShapeDtypeStruct((planes - 2, tile_y, cols), F32)
    image = jax.ShapeDtypeStruct((count, planes - 2, tile_y, cols), BF16)
    return pl.pallas_call(
        functools.partial(image_kernel, group),
        out_shape=(image, field, field),
        in_specs=[SMEM_SPEC] + [VMEM_SPEC] * 2,
        out_specs=(ANY_SPEC,) * 3,
        scratch_shapes=[
            pltpu.VMEM((2,) + own.shape, F32),
            pltpu.VMEM(image.shape, BF16),
            pltpu.SemaphoreType.DMA((count // group,)),
            pltpu.SemaphoreType.DMA((2,)),
        ],
        compiler_params=params(4 * image.size),
        name="image",
    )(lags, on_chip(own), on_chip(other))


def shards(
    vel_index,
    courant,
    src_now,
    src_prev,
    rec_now,
    rec_prev,
    src_pos,
    src_wavelet,
    rec_pos,
    rec_traces,
    offset_lags,
):
    bands, roles = lax.axis_size("band"), lax.axis_size("role")
    chips = roles // CORES
    cols = src_now.shape[2]
    partner = [(i, i + 1 - 2 * (i % CORES)) for i in range(roles)]

    pair, send = pack(vel_index, src_now, src_prev, rec_now, rec_prev)
    pair = lax.dynamic_update_index_in_dim(pair, lax.ppermute(send, "role", partner), 1, 0)
    pieces = []
    for shift in range(bands):
        moved = pair
        if shift:
            moved = lax.ppermute(pair, "band", [(i, (i + shift) % bands) for i in range(bands)])
        pieces.append(moved)
        for hop in range(1, chips):
            perm = [(i, (i + CORES * hop) % roles) for i in range(roles)]
            pieces.append(lax.ppermute(moved, "role", perm))
    late = inject(rec_pos, rec_traces, bands * src_now.shape[1], cols)
    early = lax.ppermute(late, "role", [(i, i + 1) for i in range(0, roles, CORES)])
    own, outgoing = propagate(
        pieces, bands, chips, src_wavelet, src_pos, courant[None], late, early
    )
    other = lax.ppermute(outgoing, "role", partner)
    return make_image(offset_lags, own, other)


def solution(mesh):
    field = P(("survey", "role"), "band", None)
    placed = (P("role", "band", None), P()) + (field,) * 4 + (P("survey", None),) * 4 + (P(),)
    return jax.shard_map(
        shards,
        mesh=mesh,
        in_specs=placed,
        out_specs=(P("survey", "role", "band", None), field, field),
        check_vma=False,
    )
```

time: 44.9 us -> 39.6 us (0.88)
  Pallas kernels: 23.4 us -> 14.3 us
  local copies, waits for them, and re-layouts: 1.8 us -> 4.56 us
  starting transfers between devices: 10.5 us -> 12 us
  other arithmetic: 0.79 us -> 0 us
    pallas_call x3, Pallas kernels: 11.2 us -> 6.63 us  [the longest x1 4.11 us: make_image(): pl.pallas_call(functools.partial(image_kernel, group), out_shape=(image,...]
    pallas_call x1, Pallas kernels: 12.2 us -> 7.7 us  [propagate(): pl.pallas_call(functools.partial(step_kernel, bands, chips, steps), out_s...]
    unnamed x20 -> x22, local copies, waits for them, and re-layouts: 1.28 us -> 4.55 us
    ppermute x1 -> x2, starting transfers between devices: 0.49 us -> 1.86 us  [the longest x1 1.3 us: shards(): lax.ppermute(late, 'role', [(i, i + 1) for i in range(0, roles, CORES)])]
    another operation x1 -> x0, other arithmetic: 0.79 us -> none  [shards(): pair = jnp.stack([keep, lax.ppermute(send, 'role', partner)])]
    broadcast_in_dim x1 -> x0, local copies, waits for them, and re-layouts: 0.51 us -> none  [shards(): table = jnp.pad(courant, (0, 128 - courant.shape[0]))[None]]
    ppermute x1 -> x2, waiting for transfers between devices: 1.08 us -> 0.87 us  [the longest x1 0.87 us: shards(): lax.ppermute(send, 'role', partner)]
  transfers between devices with their start and end apart: 9 -> 10, of which waited for: 6 -> 7; matrix products, arithmetic and copies ran while one was open for 1% -> 0% of each run, Pallas kernels for 12% -> 6%
where the time goes in v2:
time: 39.6 us; the launch traced here: 39 us
  Pallas kernels  14.3 us (36%)
  starting transfers between devices  12 us (30%)
  waiting for transfers between devices  7.37 us (19%)
  local copies, waits for them, and re-layouts  4.56 us (12%)
  between operations  0.71 us (2%)
    pallas_call x1, Pallas kernels, propagate(): pl.pallas_call(functools.partial(step_kernel, bands, chips, steps), out_s...  7.7 us
    ppermute x3, starting transfers between devices, shards(): lax.ppermute(pair, 'band', [(i, (i + shift) % bands) for i in range(bands)])  6 us
    ppermute x4, waiting for transfers between devices, shards(): pieces.append(lax.ppermute(moved, 'role', perm))  5.08 us
    unnamed x22, local copies, waits for them, and re-layouts  4.55 us
    ppermute x4, starting transfers between devices, shards(): pieces.append(lax.ppermute(moved, 'role', perm))  4.12 us
    pallas_call x1, Pallas kernels, make_image(): pl.pallas_call(functools.partial(image_kernel, group), out_shape=(image,...  4.11 us
    pallas_call x1, Pallas kernels, inject(): pl.pallas_call(functools.partial(inject_kernel, chunk), out_shape=pltpu.V...  2.5 us
    ppermute x1, starting transfers between devices, shards(): lax.ppermute(late, 'role', [(i, i + 1) for i in range(0, roles, CORES)])  1.3 us
  transfers between devices with their start and end apart: 10, of which 7 were waited for; matrix products, arithmetic and copies ran while one was open for 0% of the time, Pallas kernels for 6%

profile of v2, /device:TPU:0, one launch (start us, length us, event | category | flops | bytes accessed | tf_op | source)
XLA Modules:
  0.0 39.0 jit_solution(16173798089581174718)
XLA Ops:
  0.6 0.7 %copy-done.2 = s32[4,8,128]{2,1,0:T(8,128)S(1)} copy-done((s32[4,8,128]{2,1,0:T(8,128)S(1)}, s32[4,8,128]{2,1,0:T(8,128)}, u32[]{:S(2)}) %copy-start.2) | copy-done | bytes 16408
  1.4 0.7 %copy-done.3 = f32[4,8,128]{2,1,0:T(8,128)S(1)} copy-done((f32[4,8,128]{2,1,0:T(8,128)S(1)}, f32[4,8,128]{2,1,0:T(8,128)}, u32[]{:S(2)}) %copy-start.3) | copy-done | bytes 16408
  2.1 0.7 %copy-done.4 = f32[4,8,128]{2,1,0:T(8,128)S(1)} copy-done((f32[4,8,128]{2,1,0:T(8,128)S(1)}, f32[4,8,128]{2,1,0:T(8,128)}, u32[]{:S(2)}) %copy-start.4) | copy-done | bytes 16408
  2.8 0.7 %copy-done.5 = f32[4,8,128]{2,1,0:T(8,128)S(1)} copy-done((f32[4,8,128]{2,1,0:T(8,128)S(1)}, f32[4,8,128]{2,1,0:T(8,128)}, u32[]{:S(2)}) %copy-start.5) | copy-done | bytes 16408
  3.5 0.7 %copy-done.6 = f32[4,8,128]{2,1,0:T(8,128)S(1)} copy-done((f32[4,8,128]{2,1,0:T(8,128)S(1)}, f32[4,8,128]{2,1,0:T(8,128)}, u32[]{:S(2)}) %copy-start.6) | copy-done | bytes 16408
  4.2 0.6 %collective-permute-start.1 = (bf16[5,4,8,128]{3,2,1,0:T(8,128)(2,1)S(1)}, bf16[5,4,8,128]{3,2,1,0:T(8,128)(2,1)S(1)}, u32[]{:S(2)}, u32[]{:S(2)}) collective-permute-start(bf16[5,4,8,128]{3,2,1,0:T(8,128)(2,1)S(1)} %get-tuple-element.8), channel_id=1, source_target_pairs={{0,1},{1,0},{2,3},{3,2},{4,5},{5,4},{6,7},{7,6},{8,9},{9,8},{10,11... | collective-permute-start | bytes 122888 | tf_op jit(solution)/shard_map/ppermute | solution.py:391
  4.8 0.9 %collective-permute-done.1 = bf16[5,4,8,128]{3,2,1,0:T(8,128)(2,1)S(1)} collective-permute-done((bf16[5,4,8,128]{3,2,1,0:T(8,128)(2,1)S(1)}, bf16[5,4,8,128]{3,2,1,0:T(8,128)(2,1)S(1)}, u32[]{:S(2)}, u32[]{:S(2)}) %collective-permute-start.1) | collective-permute-done | bytes 40992 | tf_op jit(solution)/shard_map/ppermute | solution.py:391
  5.7 5.0 %collective-permute-start.7 = (bf16[2,5,4,8,128]{4,3,2,1,0:T(8,128)(2,1)S(1)}, bf16[2,5,4,8,128]{4,3,2,1,0:T(8,128)(2,1)S(1)}, u32[]{:S(2)}, u32[]{:S(2)}) collective-permute-start(bf16[2,5,4,8,128]{4,3,2,1,0:T(8,128)(2,1)S(1)} %bitcast_dynamic-update-slice_fusion.refs_5_), channel_id=1, source_target_pairs={{0,12},{4,0},{8,4},{12,8},{1,13},{5,1},{9,5},{13,9},{2,14},{6,2},{... | collective-permute-start | bytes 245768 | tf_op jit(solution)/shard_map/ppermute | solution.py:396
  10.7 1.0 %collective-permute-start.3 = (bf16[2,5,4,8,128]{4,3,2,1,0:T(8,128)(2,1)S(1)}, bf16[2,5,4,8,128]{4,3,2,1,0:T(8,128)(2,1)S(1)}, u32[]{:S(2)}, u32[]{:S(2)}) collective-permute-start(bf16[2,5,4,8,128]{4,3,2,1,0:T(8,128)(2,1)S(1)} %bitcast_dynamic-update-slice_fusion.refs_5_), channel_id=1, source_target_pairs={{0,4},{4,8},{8,12},{12,0},{1,5},{5,9},{9,13},{13,1},{2,6},{6,10},{... | collective-permute-start | bytes 245768 | tf_op jit(solution)/shard_map/ppermute | solution.py:396
  11.7 0.9 %copy-done = f32[4096,16]{0,1:T(8,128)S(1)} copy-done((f32[4096,16]{0,1:T(8,128)S(1)}, f32[4096,16]{0,1:T(8,128)}, u32[]{:S(2)}) %copy-start) | copy-done | bytes 262168
  12.6 2.5 %inject.1.refs_3_ = f32[8,32,128]{2,1,0:T(8,128)S(1)} custom-call(s32[2,4096]{1,0:T(2,128)S(1)} %bitcast.6, f32[16,4096]{1,0:T(8,128)S(1)} %bitcast.5), custom_call_target="tpu_custom_call" | custom-call | tf_op jit(solution)/shard_map/inject/pallas_call | solution.py:98
  15.2 1.3 %collective-permute-start = (f32[8,32,128]{2,1,0:T(8,128)S(1)}, f32[8,32,128]{2,1,0:T(8,128)S(1)}, u32[]{:S(2)}, u32[]{:S(2)}) collective-permute-start(f32[8,32,128]{2,1,0:T(8,128)S(1)} %inject.1.refs_3_), channel_id=1, source_target_pairs={{0,1},{2,3},{4,5},{6,7},{8,9},{10,11},{12,13},{14,15},{16,17},{18,... | collective-permute-start | bytes 393224 | tf_op jit(solution)/shard_map/ppermute | solution.py:402
  16.5 1.5 %collective-permute-start.2 = (bf16[2,5,4,8,128]{4,3,2,1,0:T(8,128)(2,1)S(1)}, bf16[2,5,4,8,128]{4,3,2,1,0:T(8,128)(2,1)S(1)}, u32[]{:S(2)}, u32[]{:S(2)}) collective-permute-start(bf16[2,5,4,8,128]{4,3,2,1,0:T(8,128)(2,1)S(1)} %bitcast_dynamic-update-slice_fusion.refs_5_), channel_id=1, source_target_pairs={{0,2},{1,3},{2,0},{3,1},{4,6},{5,7},{6,4},{7,5},{8,10},{9,11},{10,... | collective-permute-start | bytes 245768 | tf_op jit(solution)/shard_map/ppermute | solution.py:400
  18.0 0.5 %collective-permute-start.8 = (bf16[2,5,4,8,128]{4,3,2,1,0:T(8,128)(2,1)S(1)}, bf16[2,5,4,8,128]{4,3,2,1,0:T(8,128)(2,1)S(1)}, u32[]{:S(2)}, u32[]{:S(2)}) collective-permute-start(bf16[2,5,4,8,128]{4,3,2,1,0:T(8,128)(2,1)S(1)} %collective-permute-done.7.refs_11_), channel_id=1, source_target_pairs={{0,2},{1,3},{2,0},{3,1},{4,6},{5,7},{6,4},{7,5},{8,10},{9,11},{10,... | collective-permute-start | bytes 245768 | tf_op jit(solution)/shard_map/ppermute | solution.py:400
  18.6 0.1 collective-permute-done.5.refs_9_
  18.7 1.5 %collective-permute-start.6 = (bf16[2,5,4,8,128]{4,3,2,1,0:T(8,128)(2,1)S(1)}, bf16[2,5,4,8,128]{4,3,2,1,0:T(8,128)(2,1)S(1)}, u32[]{:S(2)}, u32[]{:S(2)}) collective-permute-start(bf16[2,5,4,8,128]{4,3,2,1,0:T(8,128)(2,1)S(1)} %collective-permute-done.5.refs_9_), channel_id=1, source_target_pairs={{0,2},{1,3},{2,0},{3,1},{4,6},{5,7},{6,4},{7,5},{8,10},{9,11},{10,... | collective-permute-start | bytes 245768 | tf_op jit(solution)/shard_map/ppermute | solution.py:400
  20.2 0.5 %collective-permute-start.4 = (bf16[2,5,4,8,128]{4,3,2,1,0:T(8,128)(2,1)S(1)}, bf16[2,5,4,8,128]{4,3,2,1,0:T(8,128)(2,1)S(1)}, u32[]{:S(2)}, u32[]{:S(2)}) collective-permute-start(bf16[2,5,4,8,128]{4,3,2,1,0:T(8,128)(2,1)S(1)} %collective-permute-done.3.refs_7_), channel_id=1, source_target_pairs={{0,2},{1,3},{2,0},{3,1},{4,6},{5,7},{6,4},{7,5},{8,10},{9,11},{10,... | collective-permute-start | bytes 245768 | tf_op jit(solution)/shard_map/ppermute | solution.py:400
  20.7 1.0 %collective-permute-done.2.refs_6_ = bf16[2,5,4,8,128]{4,3,2,1,0:T(8,128)(2,1)S(1)} collective-permute-done((bf16[2,5,4,8,128]{4,3,2,1,0:T(8,128)(2,1)S(1)}, bf16[2,5,4,8,128]{4,3,2,1,0:T(8,128)(2,1)S(1)}, u32[]{:S(2)}, u32[]{:S(2)}) %collective-permute-start.2) | collective-permute-done | bytes 81952 | tf_op jit(solution)/shard_map/ppermute | solution.py:400
  21.7 1.8 %collective-permute-done.8.refs_12_ = bf16[2,5,4,8,128]{4,3,2,1,0:T(8,128)(2,1)S(1)} collective-permute-done((bf16[2,5,4,8,128]{4,3,2,1,0:T(8,128)(2,1)S(1)}, bf16[2,5,4,8,128]{4,3,2,1,0:T(8,128)(2,1)S(1)}, u32[]{:S(2)}, u32[]{:S(2)}) %collective-permute-start.8) | collective-permute-done | bytes 81952 | tf_op jit(solution)/shard_map/ppermute | solution.py:400
  23.5 1.5 %collective-permute-done.6.refs_10_ = bf16[2,5,4,8,128]{4,3,2,1,0:T(8,128)(2,1)S(1)} collective-permute-done((bf16[2,5,4,8,128]{4,3,2,1,0:T(8,128)(2,1)S(1)}, bf16[2,5,4,8,128]{4,3,2,1,0:T(8,128)(2,1)S(1)}, u32[]{:S(2)}, u32[]{:S(2)}) %collective-permute-start.6) | collective-permute-done | bytes 81952 | tf_op jit(solution)/shard_map/ppermute | solution.py:400
  24.9 0.9 %collective-permute-done.4.refs_8_ = bf16[2,5,4,8,128]{4,3,2,1,0:T(8,128)(2,1)S(1)} collective-permute-done((bf16[2,5,4,8,128]{4,3,2,1,0:T(8,128)(2,1)S(1)}, bf16[2,5,4,8,128]{4,3,2,1,0:T(8,128)(2,1)S(1)}, u32[]{:S(2)}, u32[]{:S(2)}) %collective-permute-start.4) | collective-permute-done | bytes 81952 | tf_op jit(solution)/shard_map/ppermute | solution.py:400
  25.8 7.7 %propagate.1 = (f32[4,6,8,128]{3,2,1,0:T(8,128)S(1)}, f32[4,6,8,128]{3,2,1,0:T(8,128)S(1)}) custom-call(f32[4,16]{1,0:T(4,128)S(1)} %copy-done.7, s32[4,3]{1,0:T(4,128)S(1)} %copy-done.8, f32[1,32]{1,0:T(1,128)S(1)} %bitcast.7, f32[8,32,128]{2,1,0:T(8,128)S(1)} %inject.1.refs_3_, f32[8,32,128]{2,1,0:T(8,128)S(1)} %collective-permute-done.refs_4_, ...), custom_call_target="tpu_custom_call" | custom-call | tf_op jit(solution)/shard_map/propagate/pallas_call | solution.py:284
  33.6 1.3 %collective-permute-done.9.other_ref = f32[4,6,8,128]{3,2,1,0:T(8,128)S(1)} collective-permute-done((f32[4,6,8,128]{3,2,1,0:T(8,128)S(1)}, f32[4,6,8,128]{3,2,1,0:T(8,128)S(1)}, u32[]{:S(2)}, u32[]{:S(2)}) %collective-permute-start.9) | collective-permute-done | bytes 98336 | tf_op jit(solution)/shard_map/ppermute | solution.py:406
  34.9 4.1 %image.1 = (bf16[32,4,8,128]{3,2,1,0:T(8,128)(2,1)}, f32[4,8,128]{2,1,0:T(8,128)}, f32[4,8,128]{2,1,0:T(8,128)}) custom-call(s32[32]{0:T(128)S(1)} %copy-done.10, f32[4,6,8,128]{3,2,1,0:T(8,128)S(1)} %get-tuple-element.9.own_ref, f32[4,6,8,128]{3,2,1,0:T(8,128)S(1)} %collective-permute-done.9.other_ref), custom_call_target="tpu_custom_call" | custom-call | tf_op jit(solution)/shard_map/image/pallas_call | solution.py:356
  (23 shorter events, 0.1 us)
Async XLA Ops:
  0.6 0.7 %copy-start.2 = (s32[4,8,128]{2,1,0:T(8,128)S(1)}, s32[4,8,128]{2,1,0:T(8,128)}, u32[]{:S(2)}) copy-start(s32[4,8,128]{2,1,0:T(8,128)} %vel_ref.1) | copy-start | bytes 49156
  1.4 0.7 %copy-start.3 = (f32[4,8,128]{2,1,0:T(8,128)S(1)}, f32[4,8,128]{2,1,0:T(8,128)}, u32[]{:S(2)}) copy-start(f32[4,8,128]{2,1,0:T(8,128)} %sn_ref.1) | copy-start | bytes 49156
  2.1 0.7 %copy-start.4 = (f32[4,8,128]{2,1,0:T(8,128)S(1)}, f32[4,8,128]{2,1,0:T(8,128)}, u32[]{:S(2)}) copy-start(f32[4,8,128]{2,1,0:T(8,128)} %sp_ref.1) | copy-start | bytes 49156
  2.8 0.7 %copy-start.5 = (f32[4,8,128]{2,1,0:T(8,128)S(1)}, f32[4,8,128]{2,1,0:T(8,128)}, u32[]{:S(2)}) copy-start(f32[4,8,128]{2,1,0:T(8,128)} %rn_ref.1) | copy-start | bytes 49156
  3.5 0.7 %copy-start.6 = (f32[4,8,128]{2,1,0:T(8,128)S(1)}, f32[4,8,128]{2,1,0:T(8,128)}, u32[]{:S(2)}) copy-start(f32[4,8,128]{2,1,0:T(8,128)} %rp_ref.1) | copy-start | bytes 49156
  4.2 1.4 %collective-permute-start.1 = (bf16[5,4,8,128]{3,2,1,0:T(8,128)(2,1)S(1)}, bf16[5,4,8,128]{3,2,1,0:T(8,128)(2,1)S(1)}, u32[]{:S(2)}, u32[]{:S(2)}) collective-permute-start(bf16[5,4,8,128]{3,2,1,0:T(8,128)(2,1)S(1)} %get-tuple-element.8), channel_id=1, source_target_pairs={{0,1},{1,0},{2,3},{3,2},{4,5},{5,4},{6,7},{7,6},{8,9},{9,8},{10,11... | collective-permute-start | bytes 122888 | tf_op jit(solution)/shard_map/ppermute | solution.py:391
  5.7 6.0 %copy-start.1 = (s32[4096,2]{0,1:T(2,128)S(1)}, s32[4096,2]{0,1:T(2,128)}, u32[]{:S(2)}) copy-start(s32[4096,2]{0,1:T(2,128)} %param.19) | copy-start | bytes 98308
  5.7 12.3 %collective-permute-start.7 = (bf16[2,5,4,8,128]{4,3,2,1,0:T(8,128)(2,1)S(1)}, bf16[2,5,4,8,128]{4,3,2,1,0:T(8,128)(2,1)S(1)}, u32[]{:S(2)}, u32[]{:S(2)}) collective-permute-start(bf16[2,5,4,8,128]{4,3,2,1,0:T(8,128)(2,1)S(1)} %bitcast_dynamic-update-slice_fusion.refs_5_), channel_id=1, source_target_pairs={{0,12},{4,0},{8,4},{12,8},{1,13},{5,1},{9,5},{13,9},{2,14},{6,2},{... | collective-permute-start | bytes 245768 | tf_op jit(solution)/shard_map/ppermute | solution.py:396
  10.7 8.0 %collective-permute-start.5 = (bf16[2,5,4,8,128]{4,3,2,1,0:T(8,128)(2,1)S(1)}, bf16[2,5,4,8,128]{4,3,2,1,0:T(8,128)(2,1)S(1)}, u32[]{:S(2)}, u32[]{:S(2)}) collective-permute-start(bf16[2,5,4,8,128]{4,3,2,1,0:T(8,128)(2,1)S(1)} %bitcast_dynamic-update-slice_fusion.refs_5_), channel_id=1, source_target_pairs={{0,8},{4,12},{8,0},{12,4},{1,9},{5,13},{9,1},{13,5},{2,10},{6,14},... | collective-permute-start | bytes 245768 | tf_op jit(solution)/shard_map/ppermute | solution.py:396
  10.7 9.5 %collective-permute-start.3 = (bf16[2,5,4,8,128]{4,3,2,1,0:T(8,128)(2,1)S(1)}, bf16[2,5,4,8,128]{4,3,2,1,0:T(8,128)(2,1)S(1)}, u32[]{:S(2)}, u32[]{:S(2)}) collective-permute-start(bf16[2,5,4,8,128]{4,3,2,1,0:T(8,128)(2,1)S(1)} %bitcast_dynamic-update-slice_fusion.refs_5_), channel_id=1, source_target_pairs={{0,4},{4,8},{8,12},{12,0},{1,5},{5,9},{9,13},{13,1},{2,6},{6,10},{... | collective-permute-start | bytes 245768 | tf_op jit(solution)/shard_map/ppermute | solution.py:396
  11.7 1.0 %copy-start = (f32[4096,16]{0,1:T(8,128)S(1)}, f32[4096,16]{0,1:T(8,128)}, u32[]{:S(2)}) copy-start(f32[4096,16]{0,1:T(8,128)} %param.20) | copy-start | bytes 786436
  12.6 13.2 %copy-start.7 = (f32[4,16]{1,0:T(4,128)S(1)}, f32[4,16]{1,0:T(4,128)}, u32[]{:S(2)}) copy-start(f32[4,16]{1,0:T(4,128)} %refs_0_.1) | copy-start | bytes 772
  12.6 13.2 %copy-start.8 = (s32[4,3]{1,0:T(4,128)S(1)}, s32[4,3]{1,0:T(4,128)}, u32[]{:S(2)}) copy-start(s32[4,3]{1,0:T(4,128)} %refs_1_.1) | copy-start | bytes 148
  15.2 10.7 %copy-start.9 = (f32[32]{0:T(128)S(1)}, f32[32]{0:T(128)}, u32[]{:S(2)}) copy-start(f32[32]{0:T(128)} %param.12) | copy-start | bytes 388
  15.2 6.5 %collective-permute-start = (f32[8,32,128]{2,1,0:T(8,128)S(1)}, f32[8,32,128]{2,1,0:T(8,128)S(1)}, u32[]{:S(2)}, u32[]{:S(2)}) collective-permute-start(f32[8,32,128]{2,1,0:T(8,128)S(1)} %inject.1.refs_3_), channel_id=1, source_target_pairs={{0,1},{2,3},{4,5},{6,7},{8,9},{10,11},{12,13},{14,15},{16,17},{18,... | collective-permute-start | bytes 393224 | tf_op jit(solution)/shard_map/ppermute | solution.py:402
  16.5 5.2 %collective-permute-start.2 = (bf16[2,5,4,8,128]{4,3,2,1,0:T(8,128)(2,1)S(1)}, bf16[2,5,4,8,128]{4,3,2,1,0:T(8,128)(2,1)S(1)}, u32[]{:S(2)}, u32[]{:S(2)}) collective-permute-start(bf16[2,5,4,8,128]{4,3,2,1,0:T(8,128)(2,1)S(1)} %bitcast_dynamic-update-slice_fusion.refs_5_), channel_id=1, source_target_pairs={{0,2},{1,3},{2,0},{3,1},{4,6},{5,7},{6,4},{7,5},{8,10},{9,11},{10,... | collective-permute-start | bytes 245768 | tf_op jit(solution)/shard_map/ppermute | solution.py:400
  18.0 5.4 %collective-permute-start.8 = (bf16[2,5,4,8,128]{4,3,2,1,0:T(8,128)(2,1)S(1)}, bf16[2,5,4,8,128]{4,3,2,1,0:T(8,128)(2,1)S(1)}, u32[]{:S(2)}, u32[]{:S(2)}) collective-permute-start(bf16[2,5,4,8,128]{4,3,2,1,0:T(8,128)(2,1)S(1)} %collective-permute-done.7.refs_11_), channel_id=1, source_target_pairs={{0,2},{1,3},{2,0},{3,1},{4,6},{5,7},{6,4},{7,5},{8,10},{9,11},{10,... | collective-permute-start | bytes 245768 | tf_op jit(solution)/shard_map/ppermute | solution.py:400
  18.7 6.2 %collective-permute-start.6 = (bf16[2,5,4,8,128]{4,3,2,1,0:T(8,128)(2,1)S(1)}, bf16[2,5,4,8,128]{4,3,2,1,0:T(8,128)(2,1)S(1)}, u32[]{:S(2)}, u32[]{:S(2)}) collective-permute-start(bf16[2,5,4,8,128]{4,3,2,1,0:T(8,128)(2,1)S(1)} %collective-permute-done.5.refs_9_), channel_id=1, source_target_pairs={{0,2},{1,3},{2,0},{3,1},{4,6},{5,7},{6,4},{7,5},{8,10},{9,11},{10,... | collective-permute-start | bytes 245768 | tf_op jit(solution)/shard_map/ppermute | solution.py:400
  20.2 5.6 %collective-permute-start.4 = (bf16[2,5,4,8,128]{4,3,2,1,0:T(8,128)(2,1)S(1)}, bf16[2,5,4,8,128]{4,3,2,1,0:T(8,128)(2,1)S(1)}, u32[]{:S(2)}, u32[]{:S(2)}) collective-permute-start(bf16[2,5,4,8,128]{4,3,2,1,0:T(8,128)(2,1)S(1)} %collective-permute-done.3.refs_7_), channel_id=1, source_target_pairs={{0,2},{1,3},{2,0},{3,1},{4,6},{5,7},{6,4},{7,5},{8,10},{9,11},{10,... | collective-permute-start | bytes 245768 | tf_op jit(solution)/shard_map/ppermute | solution.py:400
  33.5 1.4 %copy-start.10 = (s32[32]{0:T(128)S(1)}, s32[32]{0:T(128)}, u32[]{:S(2)}) copy-start(s32[32]{0:T(128)} %lag_ref.1) | copy-start | bytes 388
  33.5 1.4 %collective-permute-start.9 = (f32[4,6,8,128]{3,2,1,0:T(8,128)S(1)}, f32[4,6,8,128]{3,2,1,0:T(8,128)S(1)}, u32[]{:S(2)}, u32[]{:S(2)}) collective-permute-start(f32[4,6,8,128]{3,2,1,0:T(8,128)S(1)} %get-tuple-element.10), channel_id=1, source_target_pairs={{0,1},{1,0},{2,3},{3,2},{4,5},{5,4},{6,7},{7,6},{8,9},{9,8},{10,11... | collective-permute-start | bytes 294920 | tf_op jit(solution)/shard_map/ppermute | solution.py:406

commit v3 on v2

--- a/solution.py
+++ b/solution.py
@@ -18,6 +18,7 @@
 
 VMEM_SPEC = pl.BlockSpec(memory_space=pltpu.VMEM)
 SMEM_SPEC = pl.BlockSpec(memory_space=pltpu.SMEM)
+HBM_SPEC = pl.BlockSpec(memory_space=pltpu.HBM)
 ANY_SPEC = pl.BlockSpec(memory_space=pl.ANY)
 
 
@@ -34,8 +35,21 @@
     return high, (value - high.astype(F32)).astype(BF16)
 
 
-def pack_kernel(vel_ref, sn_ref, sp_ref, rn_ref, rp_ref, pair_ref, send_ref):
+def pack_kernel(*refs):
+    fields, (pos_ref, amp_ref) = refs[:5], refs[5:7]
+    pair_ref, send_ref, own_pos_ref, own_amp_ref = refs[7:11]
+    held, sems = refs[11:16], refs[16]
     core = lax.rem(lax.axis_index("role"), CORES)
+    steps = own_amp_ref.shape[0]
+    own_steps = pl.ds(pl.multiple_of(core * steps, steps), steps)
+    moves = list(zip(fields, held))
+    moves += [(pos_ref, own_pos_ref), (amp_ref.at[own_steps], own_amp_ref)]
+    copies = [pltpu.make_async_copy(a, b, sems.at[k]) for k, (a, b) in enumerate(moves)]
+    for copy in copies:
+        copy.start()
+    for copy in copies[:5]:
+        copy.wait()
+    vel_ref, sn_ref, sp_ref, rn_ref, rp_ref = held
     entry = vel_ref[...].astype(F32).astype(BF16)
     src_now, rec_now = sn_ref[...], rn_ref[...]
     src_step, rec_step = src_now - sp_ref[...], rec_now - rp_ref[...]
@@ -45,24 +59,35 @@
         out_ref[0], out_ref[1] = split(now)
         out_ref[2], out_ref[3] = split(step)
         out_ref[4] = entry
-
-
-def pack(vel_index, src_now, src_prev, rec_now, rec_prev):
+    for copy in copies[5:]:
+        copy.wait()
+
+
+def pack(vel_index, src_now, src_prev, rec_now, rec_prev, rec_pos, rec_traces):
     shape = (PARTS,) + src_now.shape
+    count, steps = rec_traces.shape
+    held = pltpu.VMEM(src_now.shape, F32)
     return pl.pallas_call(
         pack_kernel,
-        out_shape=(pltpu.VMEM((CORES,) + shape, BF16), pltpu.VMEM(shape, BF16)),
-        in_specs=[VMEM_SPEC] * 5,
-        out_specs=(VMEM_SPEC, VMEM_SPEC),
+        out_shape=(
+            pltpu.VMEM((CORES,) + shape, BF16),
+            pltpu.VMEM(shape, BF16),
+            pltpu.VMEM((2, count), jnp.int32),
+            pltpu.VMEM((steps // CORES, count), F32),
+        ),
+        in_specs=[HBM_SPEC] * 7,
+        out_specs=(VMEM_SPEC,) * 4,
+        scratch_shapes=[pltpu.VMEM(src_now.shape, jnp.int32)]
+        + [held] * 4
+        + [pltpu.SemaphoreType.DMA((7,))],
         compiler_params=params(0),
         name="pack",
-    )(vel_index, src_now, src_prev, rec_now, rec_prev)
+    )(vel_index, src_now, src_prev, rec_now, rec_prev, rec_pos.T, rec_traces.T)
 
 
 def inject_kernel(chunk, pos_ref, amp_ref, out_ref, acc_ref):
     count = amp_ref.shape[1]
     steps, rows, cols = out_ref.shape
-    own = pl.ds(pl.multiple_of(lax.rem(lax.axis_index("role"), CORES) * steps, steps), steps)
     acc_ref[...] = jnp.zeros_like(acc_ref)
 
     def one(at, carry):
@@ -71,7 +96,7 @@
         in_row = lax.broadcasted_iota(jnp.int32, (rows, chunk), 0) == pos[0:1]
         in_col = lax.broadcasted_iota(jnp.int32, (cols, chunk), 0) == pos[1:2]
         col_hot = jnp.where(in_col, 1.0, 0.0).astype(BF16)
-        amp = amp_ref[own, span]
+        amp = amp_ref[:, span]
         high = amp.astype(BF16).astype(F32)
         total = None
         for part in (high, amp - high):
@@ -90,20 +115,23 @@
         out_ref[k] = acc_ref[k * rows : (k + 1) * rows]
 
 
-def inject(rec_pos, rec_traces, rows, cols):
-    count, steps = rec_traces.shape
-    own_steps = steps // CORES
+def inject(own_pos, own_amp, rows, cols):
+    steps, count = own_amp.shape
     chunk = next(c for c in (512, 256, 128, count) if count % c == 0)
-    scratch = own_steps * rows * cols * 4
+    scratch = steps * rows * cols * 4
     return pl.pallas_call(
         functools.partial(inject_kernel, chunk),
-        out_shape=pltpu.VMEM((own_steps, rows, cols), F32),
+        out_shape=pltpu.VMEM((steps, rows, cols), F32),
         in_specs=[VMEM_SPEC] * 2,
         out_specs=VMEM_SPEC,
-        scratch_shapes=[pltpu.VMEM((own_steps * rows, cols), F32)],
+        scratch_shapes=[pltpu.VMEM((steps * rows, cols), F32)],
         compiler_params=params(6 * scratch),
         name="inject",
-    )(on_chip(rec_pos.T), on_chip(rec_traces.T))
+    )(on_chip(own_pos), on_chip(own_amp))
+
+
+def across(at, shift, count):
+    return at ^ shift if count & (count - 1) == 0 else (at + count - shift) % count
 
 
 def lookup(table, entry):
@@ -128,7 +156,7 @@
     wavelet_ref, src_pos_ref, courant_ref, late_ref, early_ref = refs[:5]
     piece_refs = refs[5 : 5 + bands * chips]
     keep_ref, send_ref = refs[5 + bands * chips : 7 + bands * chips]
-    one_ref, two_ref, speed_ref, row_ref, table_ref, mix_ref, one_split, two_split = refs[
+    one_ref, two_ref, speed_ref, row_ref, table_ref, mix_ref, parts_ref, inline_ref = refs[
         7 + bands * chips :
     ]
     _, _, tile_z, tile_y, cols = piece_refs[0].shape
@@ -159,7 +187,7 @@
     )
     table = table_ref[...]
     for shift in range(bands):
-        from_band = lax.rem(band + (bands - shift), bands)
+        from_band = across(band, shift, bands)
         y0 = pl.multiple_of(from_band * tile_y, tile_y)
         for hop in range(chips):
             from_chip = lax.rem(chip + (chips - hop), chips)
@@ -177,7 +205,7 @@
     lane = lax.broadcasted_iota(jnp.int32, (1, cols), 1)
     for i in range(sources):
         speed_row = speed_ref[src_pos_ref[i, 0], pl.ds(src_pos_ref[i, 1], 1)]
-        row_ref[pl.ds(i, 1)] = jnp.where(lane == src_pos_ref[i, 2], speed_row, 0.0)
+        row_ref[pl.ds(i, 1)] = jnp.where((lane == src_pos_ref[i, 2]) & is_source, speed_row, 0.0)
 
     def over_tiles(do):
         if unroll:
@@ -191,56 +219,51 @@
 
             lax.fori_loop(0, tiles, one_tile, 0)
 
-    def rows_of(y0, count):
-        return pl.ds(y0 * depth if unroll else pl.multiple_of(y0 * depth, 8 * depth), count)
-
-    def store_split(split_ref, y0, z, two_planes):
+    def rows_of(y0, z, planes):
+        start = y0 * depth + z * 8
+        return pl.ds(start if unroll else pl.multiple_of(start, 8), planes * 8)
+
+    def store_parts(z, two_planes):
         high, low = split(two_planes)
-        start = y0 * depth + z * 8
-        at = pl.ds(start if unroll else pl.multiple_of(start, 16), 16)
-        split_ref[at, 0:cols] = high
-        split_ref[at, cols:] = low
+        parts_ref[z * 8 : z * 8 + 16, 0:cols] = high
+        parts_ref[z * 8 : z * 8 + 16, cols:] = low
+
+    def sum_inline(y0):
+        sums = lax.dot_general(
+            parts_ref[...], mix_ref[...], (((1,), (0,)), ((), ())), preferred_element_type=F32
+        )
+        inline_ref[rows_of(y0, 0, depth)] = sums[:, 0:cols] + sums[:, cols:]
 
     def beside(ref, z, y0, distance):
         if unroll:
             return ref[z + 1, pl.ds(y0 + 8 + distance, 8)]
         return ref[z + 1, pl.ds(y0, 24)][8 + distance : 16 + distance]
 
-    def first_split(y0):
+    def first_inline(y0):
         for z in range(0, depth, 2):
             planes = [one_ref[z + k + 1, pl.ds(y0 + 8, 8)] for k in range(2)]
-            store_split(one_split, y0, z, jnp.concatenate(planes, axis=0))
-
-    over_tiles(first_split)
-
-    def advance(now_ref, now_split, new_ref, new_split, tick):
-        @pl.when(is_source)
-        def _():
-            for i in range(sources):
-                at = (src_pos_ref[i, 0] + 1, pl.ds(src_pos_ref[i, 1] + 8, 1))
-                new_ref[at] = new_ref[at] - wavelet_ref[i, tick] * row_ref[pl.ds(i, 1)]
-
-        @pl.when(jnp.logical_not(is_source))
-        def _():
-            half = late_ref.shape[0]
-            at = lax.rem(tick, half)
-            added = jnp.where(tick < half, early_ref[at], late_ref[at])
-            new_ref[1, 8 : rows + 8] = new_ref[1, 8 : rows + 8] - speed_ref[0] * added
+            store_parts(z, jnp.concatenate(planes, axis=0))
+        sum_inline(y0)
+
+    over_tiles(first_inline)
+
+    def advance(now_ref, new_ref, tick):
+        half = late_ref.shape[0]
+        turn = lax.rem(tick, half)
+        added = jnp.where(tick < half, early_ref[turn], late_ref[turn])
+        added = jnp.where(is_source, 0.0, speed_ref[0] * added)
+        new_ref[1, 8 : rows + 8] = new_ref[1, 8 : rows + 8] - added
+        for i in range(sources):
+            at = (src_pos_ref[i, 0] + 1, pl.ds(src_pos_ref[i, 1] + 8, 1))
+            new_ref[at] = new_ref[at] - wavelet_ref[i, tick] * row_ref[pl.ds(i, 1)]
 
         def stencil(y0):
-            inline = lax.dot_general(
-                now_split[rows_of(y0, 8 * depth)],
-                mix_ref[...],
-                (((1,), (0,)), ((), ())),
-                preferred_element_type=F32,
-            )
-            inline = inline[:, 0:cols] + inline[:, cols:]
             mids = [None] * 4 + [now_ref[z + 1, pl.ds(y0 + 8, 8)] for z in range(4)]
             planes = []
             for z in range(depth):
                 mids.append(now_ref[z + 5, pl.ds(y0 + 8, 8)] if z + 4 < depth else None)
                 mid = mids[4]
-                total = (3.0 * STENCIL_WEIGHTS[0]) * mid + inline[z * 8 : z * 8 + 8]
+                total = (3.0 * STENCIL_WEIGHTS[0]) * mid + inline_ref[rows_of(y0, z, 1)]
                 for j in range(1, 5):
                     pairs = beside(now_ref, z, y0, j) + beside(now_ref, z, y0, -j)
                     for near in (mids[4 - j], mids[4 + j]):
@@ -253,21 +276,22 @@
                 new_ref[z + 1, pl.ds(y0 + 8, 8)] = new
                 planes.append(new)
                 if len(planes) == 2:
-                    store_split(new_split, y0, z - 1, jnp.concatenate(planes, axis=0))
+                    store_parts(z - 1, jnp.concatenate(planes, axis=0))
                     planes = []
+            sum_inline(y0)
 
         over_tiles(stencil)
 
     y_own = pl.ds(pl.multiple_of(band * tile_y, tile_y) + 8, tile_y)
 
     def image_time(snapshot, carry):
-        fields = ((one_ref, one_split), (two_ref, two_split))
+        fields = (one_ref, two_ref)
         for substep in range(SUB):
-            now, new = fields[substep % 2], fields[1 - substep % 2]
-            advance(*now, *new, snapshot * SUB + substep)
+            now_ref, new_ref = fields[substep % 2], fields[1 - substep % 2]
+            advance(now_ref, new_ref, snapshot * SUB + substep)
         for out_ref, owner in ((keep_ref, role), (send_ref, chip * CORES + (1 - core))):
             for z in range(tile_z + 2):
-                out_ref[snapshot, z] = fields[SUB % 2][0][owner * tile_z + z, y_own]
+                out_ref[snapshot, z] = fields[SUB % 2][owner * tile_z + z, y_own]
         return carry
 
     lax.fori_loop(0, steps // SUB, image_time, 0)
@@ -279,7 +303,6 @@
     steps = wavelet.shape[1]
     snaps = pltpu.VMEM((steps // SUB, tile_z + 2, tile_y, cols), F32)
     field = pltpu.VMEM((depth + 2, rows + 16, cols), F32)
-    parted = pltpu.VMEM((depth * rows, 2 * cols), BF16)
     scratch = 4 * cols * (2 * (depth + 2) * (rows + 16) + 3 * depth * rows + 4 * cols)
     return pl.pallas_call(
         functools.partial(step_kernel, bands, chips, steps),
@@ -293,8 +316,8 @@
             pltpu.VMEM((max(8, src_pos.shape[0]), cols), F32),
             pltpu.VMEM((tile_y, 128), F32),
             pltpu.VMEM((2 * cols, 2 * cols), BF16),
-            parted,
-            parted,
+            pltpu.VMEM((depth * 8, 2 * cols), BF16),
+            pltpu.VMEM((depth * rows, cols), F32),
         ],
         compiler_params=params(scratch),
         name="propagate",
@@ -302,7 +325,7 @@
 
 
 def image_kernel(group, lag_ref, own_ref, other_ref, image_ref, src_ref, rec_ref, *scratch):
-    fields_ref, sums_ref, image_sems, field_sems = scratch
+    fields_ref, parts_ref, sums_ref, image_sems, field_sems = scratch
     is_source = lax.rem(lax.axis_index("role"), CORES) == 0
     images, planes, tile_y, cols = own_ref.shape
     for i in range(images):
@@ -318,31 +341,43 @@
             )
         )
         copies[-1].start()
-    lanes = lax.broadcasted_iota(jnp.int32, (tile_y, cols), 1)
-    for slot in range(lag_ref.shape[0]):
-        lag = lag_ref[slot]
-        reach = jnp.abs(lag)
-        there = lax.rem(2 * cols - 2 * lag, cols)
-        back = lax.rem(cols + lag, cols)
-        sums = []
-        for z in range(planes):
-            total = None
-            for i in range(images):
-                term = fields_ref[0, i, z] * pltpu.roll(fields_ref[1, i, z], there, 1)
-                total = term if total is None else total + term
-            sums.append(total)
-        inside = (lanes >= reach) & (lanes < cols - reach)
-        for z in range(planes - 2):
-            value = (2.0 * sums[z + 1] - sums[z]) - sums[z + 2]
-            sums_ref[slot, z] = jnp.where(inside, pltpu.roll(value, back, 1), 0.0).astype(BF16)
-        if (slot + 1) % group == 0:
-            at = pl.ds(slot + 1 - group, group)
-            copies.append(
-                pltpu.make_async_copy(
-                    sums_ref.at[at], image_ref.at[at], image_sems.at[slot // group]
+    high, low = split(fields_ref[1].reshape(images * planes * tile_y, cols))
+    parts_ref[:, 0:cols] = high
+    parts_ref[:, cols:] = low
+    ahead = lax.broadcasted_iota(jnp.int32, (cols, cols), 0)
+    ahead = ahead - lax.broadcasted_iota(jnp.int32, (cols, cols), 1)
+    for first in range(0, lag_ref.shape[0], 2):
+        slots = (first, first + 1)
+        moves = [jnp.where(ahead == 2 * lag_ref[h], 1.0, 0.0).astype(BF16) for h in slots]
+        moves = jnp.concatenate(moves, axis=1)
+        moved = lax.dot_general(
+            parts_ref[...],
+            jnp.concatenate([moves, moves], axis=0),
+            (((1,), (0,)), ((), ())),
+            preferred_element_type=F32,
+        )
+        for at, slot in enumerate(slots):
+            sums = []
+            for z in range(planes):
+                total = None
+                for i in range(images):
+                    row = (i * planes + z) * tile_y
+                    ahead_of = moved[row : row + tile_y, at * cols : (at + 1) * cols]
+                    term = fields_ref[0, i, z] * ahead_of
+                    total = term if total is None else total + term
+                sums.append(total)
+            back = lax.rem(cols + lag_ref[slot], cols)
+            for z in range(planes - 2):
+                value = (2.0 * sums[z + 1] - sums[z]) - sums[z + 2]
+                sums_ref[slot, z] = pltpu.roll(value, back, 1).astype(BF16)
+            if (slot + 1) % group == 0:
+                span = pl.ds(slot + 1 - group, group)
+                copies.append(
+                    pltpu.make_async_copy(
+                        sums_ref.at[span], image_ref.at[span], image_sems.at[slot // group]
+                    )
                 )
-            )
-            copies[-1].start()
+                copies[-1].start()
     for copy in copies:
         copy.wait()
 
@@ -360,11 +395,12 @@
         out_specs=(ANY_SPEC,) * 3,
         scratch_shapes=[
             pltpu.VMEM((2,) + own.shape, F32),
+            pltpu.VMEM((images * planes * tile_y, 2 * cols), BF16),
             pltpu.VMEM(image.shape, BF16),
             pltpu.SemaphoreType.DMA((count // group,)),
             pltpu.SemaphoreType.DMA((2,)),
         ],
-        compiler_params=params(4 * image.size),
+        compiler_params=params(4 * image.size + 64 * cols * cols),
         name="image",
     )(lags, on_chip(own), on_chip(other))
 
@@ -387,18 +423,21 @@
     cols = src_now.shape[2]
     partner = [(i, i + 1 - 2 * (i % CORES)) for i in range(roles)]
 
-    pair, send = pack(vel_index, src_now, src_prev, rec_now, rec_prev)
+    pair, send, own_pos, own_amp = pack(
+        vel_index, src_now, src_prev, rec_now, rec_prev, rec_pos, rec_traces
+    )
     pair = lax.dynamic_update_index_in_dim(pair, lax.ppermute(send, "role", partner), 1, 0)
     pieces = []
     for shift in range(bands):
         moved = pair
         if shift:
-            moved = lax.ppermute(pair, "band", [(i, (i + shift) % bands) for i in range(bands)])
+            swap = [(across(i, shift, bands), i) for i in range(bands)]
+            moved = lax.ppermute(pair, "band", swap)
         pieces.append(moved)
         for hop in range(1, chips):
             perm = [(i, (i + CORES * hop) % roles) for i in range(roles)]
             pieces.append(lax.ppermute(moved, "role", perm))
-    late = inject(rec_pos, rec_traces, bands * src_now.shape[1], cols)
+    late = inject(own_pos, own_amp, bands * src_now.shape[1], cols)
     early = lax.ppermute(late, "role", [(i, i + 1) for i in range(0, roles, CORES)])
     own, outgoing = propagate(
         pieces, bands, chips, src_wavelet, src_pos, courant[None], late, early

time: 39.6 us -> 37.9 us (0.957)
  Pallas kernels: 14.3 us -> 12 us
  local copies, waits for them, and re-layouts: 4.56 us -> 5.31 us
    pallas_call x1, Pallas kernels: 4.11 us -> 1.92 us  [make_image(): pl.pallas_call(functools.partial(image_kernel, group), out_shape=(image,...]
    unnamed x22, local copies, waits for them, and re-layouts: 4.55 us -> 5.3 us
    pallas_call x1, Pallas kernels: 7.7 us -> 7.23 us  [propagate(): pl.pallas_call(functools.partial(step_kernel, bands, chips, steps), out_s...]
  transfers between devices with their start and end apart: 10 -> 10, of which waited for: 7 -> 7; matrix products, arithmetic and copies ran while one was open for 0% -> 0% of each run, Pallas kernels for 6% -> 7%
where the time goes in v3:
time: 37.9 us; the launch traced here: 37.3 us
  Pallas kernels  12 us (32%)
  starting transfers between devices  11.8 us (31%)
  waiting for transfers between devices  7.44 us (20%)
  local copies, waits for them, and re-layouts  5.31 us (14%)
  between operations  0.71 us (2%)
    pallas_call x1, Pallas kernels, propagate(): pl.pallas_call(functools.partial(step_kernel, bands, chips, steps), out_s...  7.23 us
    ppermute x3, starting transfers between devices, shards(): moved = lax.ppermute(pair, 'band', swap)  5.63 us
    unnamed x22, local copies, waits for them, and re-layouts  5.3 us
    ppermute x4, waiting for transfers between devices, shards(): pieces.append(lax.ppermute(moved, 'role', perm))  4.85 us
    ppermute x4, starting transfers between devices, shards(): pieces.append(lax.ppermute(moved, 'role', perm))  4.12 us
    pallas_call x1, Pallas kernels, inject(): pl.pallas_call(functools.partial(inject_kernel, chunk), out_shape=pltpu.V...  2.49 us
    pallas_call x1, Pallas kernels, make_image(): pl.pallas_call(functools.partial(image_kernel, group), out_shape=(image,...  1.92 us
    ppermute x1, starting transfers between devices, shards(): lax.ppermute(late, 'role', [(i, i + 1) for i in range(0, roles, CORES)])  1.45 us
  transfers between devices with their start and end apart: 10, of which 7 were waited for; matrix products, arithmetic and copies ran while one was open for 0% of the time, Pallas kernels for 7%

profile of v3, /device:TPU:0, one launch (start us, length us, event | category | flops | bytes accessed | tf_op | source)
XLA Modules:
  0.0 37.3 jit_solution(18188639133430222974)
XLA Ops:
  0.6 0.9 %copy-done = f32[4096,16]{0,1:T(8,128)S(1)} copy-done((f32[4096,16]{0,1:T(8,128)S(1)}, f32[4096,16]{0,1:T(8,128)}, u32[]{:S(2)}) %copy-start) | copy-done | bytes 262168
  1.6 0.8 %copy-done.1 = s32[4096,2]{0,1:T(2,128)S(1)} copy-done((s32[4096,2]{0,1:T(2,128)S(1)}, s32[4096,2]{0,1:T(2,128)}, u32[]{:S(2)}) %copy-start.1) | copy-done | bytes 32792
  2.3 0.7 %copy-done.2 = s32[4,8,128]{2,1,0:T(8,128)S(1)} copy-done((s32[4,8,128]{2,1,0:T(8,128)S(1)}, s32[4,8,128]{2,1,0:T(8,128)}, u32[]{:S(2)}) %copy-start.2) | copy-done | bytes 16408
  3.1 0.7 %copy-done.3 = f32[4,8,128]{2,1,0:T(8,128)S(1)} copy-done((f32[4,8,128]{2,1,0:T(8,128)S(1)}, f32[4,8,128]{2,1,0:T(8,128)}, u32[]{:S(2)}) %copy-start.3) | copy-done | bytes 16408
  3.8 0.7 %copy-done.4 = f32[4,8,128]{2,1,0:T(8,128)S(1)} copy-done((f32[4,8,128]{2,1,0:T(8,128)S(1)}, f32[4,8,128]{2,1,0:T(8,128)}, u32[]{:S(2)}) %copy-start.4) | copy-done | bytes 16408
  4.5 0.7 %copy-done.5 = f32[4,8,128]{2,1,0:T(8,128)S(1)} copy-done((f32[4,8,128]{2,1,0:T(8,128)S(1)}, f32[4,8,128]{2,1,0:T(8,128)}, u32[]{:S(2)}) %copy-start.5) | copy-done | bytes 16408
  5.2 0.7 %copy-done.6 = f32[4,8,128]{2,1,0:T(8,128)S(1)} copy-done((f32[4,8,128]{2,1,0:T(8,128)S(1)}, f32[4,8,128]{2,1,0:T(8,128)}, u32[]{:S(2)}) %copy-start.6) | copy-done | bytes 16408
  6.3 0.6 %collective-permute-start.1 = (bf16[5,4,8,128]{3,2,1,0:T(8,128)(2,1)S(1)}, bf16[5,4,8,128]{3,2,1,0:T(8,128)(2,1)S(1)}, u32[]{:S(2)}, u32[]{:S(2)}) collective-permute-start(bf16[5,4,8,128]{3,2,1,0:T(8,128)(2,1)S(1)} %get-tuple-element.12), channel_id=1, source_target_pairs={{0,1},{1,0},{2,3},{3,2},{4,5},{5,4},{6,7},{7,6},{8,9},{9,8},{10,11... | collective-permute-start | bytes 122888 | tf_op jit(solution)/shard_map/ppermute | solution.py:429
  6.9 0.9 %collective-permute-done.1 = bf16[5,4,8,128]{3,2,1,0:T(8,128)(2,1)S(1)} collective-permute-done((bf16[5,4,8,128]{3,2,1,0:T(8,128)(2,1)S(1)}, bf16[5,4,8,128]{3,2,1,0:T(8,128)(2,1)S(1)}, u32[]{:S(2)}, u32[]{:S(2)}) %collective-permute-start.1) | collective-permute-done | bytes 40992 | tf_op jit(solution)/shard_map/ppermute | solution.py:429
  7.8 5.0 %collective-permute-start.7 = (bf16[2,5,4,8,128]{4,3,2,1,0:T(8,128)(2,1)S(1)}, bf16[2,5,4,8,128]{4,3,2,1,0:T(8,128)(2,1)S(1)}, u32[]{:S(2)}, u32[]{:S(2)}) collective-permute-start(bf16[2,5,4,8,128]{4,3,2,1,0:T(8,128)(2,1)S(1)} %bitcast_dynamic-update-slice_fusion.refs_5_), channel_id=1, source_target_pairs={{12,0},{8,4},{4,8},{0,12},{13,1},{9,5},{5,9},{1,13},{14,2},{10,6},... | collective-permute-start | bytes 245768 | tf_op jit(solution)/shard_map/ppermute | solution.py:435
  12.7 0.6 %collective-permute-start.3 = (bf16[2,5,4,8,128]{4,3,2,1,0:T(8,128)(2,1)S(1)}, bf16[2,5,4,8,128]{4,3,2,1,0:T(8,128)(2,1)S(1)}, u32[]{:S(2)}, u32[]{:S(2)}) collective-permute-start(bf16[2,5,4,8,128]{4,3,2,1,0:T(8,128)(2,1)S(1)} %bitcast_dynamic-update-slice_fusion.refs_5_), channel_id=1, source_target_pairs={{4,0},{0,4},{12,8},{8,12},{5,1},{1,5},{13,9},{9,13},{6,2},{2,6},{1... | collective-permute-start | bytes 245768 | tf_op jit(solution)/shard_map/ppermute | solution.py:435
  13.4 2.5 %inject.1.refs_3_ = f32[8,32,128]{2,1,0:T(8,128)S(1)} custom-call(s32[2,4096]{1,0:T(2,128)S(1)} %get-tuple-element.9.pos_ref, f32[8,4096]{1,0:T(8,128)S(1)} %get-tuple-element.10.amp_ref), custom_call_target="tpu_custom_call" | custom-call | tf_op jit(solution)/shard_map/inject/pallas_call | solution.py:122
  15.9 1.4 %collective-permute-start = (f32[8,32,128]{2,1,0:T(8,128)S(1)}, f32[8,32,128]{2,1,0:T(8,128)S(1)}, u32[]{:S(2)}, u32[]{:S(2)}) collective-permute-start(f32[8,32,128]{2,1,0:T(8,128)S(1)} %inject.1.refs_3_), channel_id=1, source_target_pairs={{0,1},{2,3},{4,5},{6,7},{8,9},{10,11},{12,13},{14,15},{16,17},{18,... | collective-permute-start | bytes 393224 | tf_op jit(solution)/shard_map/ppermute | solution.py:441
  17.4 1.6 %collective-permute-start.2 = (bf16[2,5,4,8,128]{4,3,2,1,0:T(8,128)(2,1)S(1)}, bf16[2,5,4,8,128]{4,3,2,1,0:T(8,128)(2,1)S(1)}, u32[]{:S(2)}, u32[]{:S(2)}) collective-permute-start(bf16[2,5,4,8,128]{4,3,2,1,0:T(8,128)(2,1)S(1)} %bitcast_dynamic-update-slice_fusion.refs_5_), channel_id=1, source_target_pairs={{0,2},{1,3},{2,0},{3,1},{4,6},{5,7},{6,4},{7,5},{8,10},{9,11},{10,... | collective-permute-start | bytes 245768 | tf_op jit(solution)/shard_map/ppermute | solution.py:439
  18.9 0.5 %collective-permute-start.8 = (bf16[2,5,4,8,128]{4,3,2,1,0:T(8,128)(2,1)S(1)}, bf16[2,5,4,8,128]{4,3,2,1,0:T(8,128)(2,1)S(1)}, u32[]{:S(2)}, u32[]{:S(2)}) collective-permute-start(bf16[2,5,4,8,128]{4,3,2,1,0:T(8,128)(2,1)S(1)} %collective-permute-done.7.refs_11_), channel_id=1, source_target_pairs={{0,2},{1,3},{2,0},{3,1},{4,6},{5,7},{6,4},{7,5},{8,10},{9,11},{10,... | collective-permute-start | bytes 245768 | tf_op jit(solution)/shard_map/ppermute | solution.py:439
  19.9 1.5 %collective-permute-start.6 = (bf16[2,5,4,8,128]{4,3,2,1,0:T(8,128)(2,1)S(1)}, bf16[2,5,4,8,128]{4,3,2,1,0:T(8,128)(2,1)S(1)}, u32[]{:S(2)}, u32[]{:S(2)}) collective-permute-start(bf16[2,5,4,8,128]{4,3,2,1,0:T(8,128)(2,1)S(1)} %collective-permute-done.5.refs_9_), channel_id=1, source_target_pairs={{0,2},{1,3},{2,0},{3,1},{4,6},{5,7},{6,4},{7,5},{8,10},{9,11},{10,... | collective-permute-start | bytes 245768 | tf_op jit(solution)/shard_map/ppermute | solution.py:439
  21.4 0.5 %collective-permute-start.4 = (bf16[2,5,4,8,128]{4,3,2,1,0:T(8,128)(2,1)S(1)}, bf16[2,5,4,8,128]{4,3,2,1,0:T(8,128)(2,1)S(1)}, u32[]{:S(2)}, u32[]{:S(2)}) collective-permute-start(bf16[2,5,4,8,128]{4,3,2,1,0:T(8,128)(2,1)S(1)} %collective-permute-done.3.refs_7_), channel_id=1, source_target_pairs={{0,2},{1,3},{2,0},{3,1},{4,6},{5,7},{6,4},{7,5},{8,10},{9,11},{10,... | collective-permute-start | bytes 245768 | tf_op jit(solution)/shard_map/ppermute | solution.py:439
  21.9 0.8 %collective-permute-done.2.refs_6_ = bf16[2,5,4,8,128]{4,3,2,1,0:T(8,128)(2,1)S(1)} collective-permute-done((bf16[2,5,4,8,128]{4,3,2,1,0:T(8,128)(2,1)S(1)}, bf16[2,5,4,8,128]{4,3,2,1,0:T(8,128)(2,1)S(1)}, u32[]{:S(2)}, u32[]{:S(2)}) %collective-permute-start.2) | collective-permute-done | bytes 81952 | tf_op jit(solution)/shard_map/ppermute | solution.py:439
  22.7 1.8 %collective-permute-done.8.refs_12_ = bf16[2,5,4,8,128]{4,3,2,1,0:T(8,128)(2,1)S(1)} collective-permute-done((bf16[2,5,4,8,128]{4,3,2,1,0:T(8,128)(2,1)S(1)}, bf16[2,5,4,8,128]{4,3,2,1,0:T(8,128)(2,1)S(1)}, u32[]{:S(2)}, u32[]{:S(2)}) %collective-permute-start.8) | collective-permute-done | bytes 81952 | tf_op jit(solution)/shard_map/ppermute | solution.py:439
  24.5 1.4 %collective-permute-done.6.refs_10_ = bf16[2,5,4,8,128]{4,3,2,1,0:T(8,128)(2,1)S(1)} collective-permute-done((bf16[2,5,4,8,128]{4,3,2,1,0:T(8,128)(2,1)S(1)}, bf16[2,5,4,8,128]{4,3,2,1,0:T(8,128)(2,1)S(1)}, u32[]{:S(2)}, u32[]{:S(2)}) %collective-permute-start.6) | collective-permute-done | bytes 81952 | tf_op jit(solution)/shard_map/ppermute | solution.py:439
  25.9 0.9 %collective-permute-done.4.refs_8_ = bf16[2,5,4,8,128]{4,3,2,1,0:T(8,128)(2,1)S(1)} collective-permute-done((bf16[2,5,4,8,128]{4,3,2,1,0:T(8,128)(2,1)S(1)}, bf16[2,5,4,8,128]{4,3,2,1,0:T(8,128)(2,1)S(1)}, u32[]{:S(2)}, u32[]{:S(2)}) %collective-permute-start.4) | collective-permute-done | bytes 81952 | tf_op jit(solution)/shard_map/ppermute | solution.py:439
  26.8 7.2 %propagate.1 = (f32[4,6,8,128]{3,2,1,0:T(8,128)S(1)}, f32[4,6,8,128]{3,2,1,0:T(8,128)S(1)}) custom-call(f32[4,16]{1,0:T(4,128)S(1)} %copy-done.7, s32[4,3]{1,0:T(4,128)S(1)} %copy-done.8, f32[1,32]{1,0:T(1,128)S(1)} %bitcast.7, f32[8,32,128]{2,1,0:T(8,128)S(1)} %inject.1.refs_3_, f32[8,32,128]{2,1,0:T(8,128)S(1)} %collective-permute-done.refs_4_, ...), custom_call_target="tpu_custom_call" | custom-call | tf_op jit(solution)/shard_map/propagate/pallas_call | solution.py:307
  34.1 1.3 %collective-permute-done.9.other_ref = f32[4,6,8,128]{3,2,1,0:T(8,128)S(1)} collective-permute-done((f32[4,6,8,128]{3,2,1,0:T(8,128)S(1)}, f32[4,6,8,128]{3,2,1,0:T(8,128)S(1)}, u32[]{:S(2)}, u32[]{:S(2)}) %collective-permute-start.9) | collective-permute-done | bytes 98336 | tf_op jit(solution)/shard_map/ppermute | solution.py:445
  35.4 1.9 %image.1 = (bf16[32,4,8,128]{3,2,1,0:T(8,128)(2,1)}, f32[4,8,128]{2,1,0:T(8,128)}, f32[4,8,128]{2,1,0:T(8,128)}) custom-call(s32[32]{0:T(128)S(1)} %copy-done.10, f32[4,6,8,128]{3,2,1,0:T(8,128)S(1)} %get-tuple-element.13.own_ref, f32[4,6,8,128]{3,2,1,0:T(8,128)S(1)} %collective-permute-done.9.other_ref), custom_call_target="tpu_custom_call" | custom-call | tf_op jit(solution)/shard_map/image/pallas_call | solution.py:391
  (23 shorter events, 0.9 us)
Async XLA Ops:
  0.6 1.0 %copy-start = (f32[4096,16]{0,1:T(8,128)S(1)}, f32[4096,16]{0,1:T(8,128)}, u32[]{:S(2)}) copy-start(f32[4096,16]{0,1:T(8,128)} %param.20) | copy-start | bytes 786436
  1.6 0.8 %copy-start.1 = (s32[4096,2]{0,1:T(2,128)S(1)}, s32[4096,2]{0,1:T(2,128)}, u32[]{:S(2)}) copy-start(s32[4096,2]{0,1:T(2,128)} %param.19) | copy-start | bytes 98308
  2.3 0.7 %copy-start.2 = (s32[4,8,128]{2,1,0:T(8,128)S(1)}, s32[4,8,128]{2,1,0:T(8,128)}, u32[]{:S(2)}) copy-start(s32[4,8,128]{2,1,0:T(8,128)} %refs_0_.2) | copy-start | bytes 49156
  3.1 0.7 %copy-start.3 = (f32[4,8,128]{2,1,0:T(8,128)S(1)}, f32[4,8,128]{2,1,0:T(8,128)}, u32[]{:S(2)}) copy-start(f32[4,8,128]{2,1,0:T(8,128)} %refs_1_.2) | copy-start | bytes 49156
  3.8 0.7 %copy-start.4 = (f32[4,8,128]{2,1,0:T(8,128)S(1)}, f32[4,8,128]{2,1,0:T(8,128)}, u32[]{:S(2)}) copy-start(f32[4,8,128]{2,1,0:T(8,128)} %refs_2_.1) | copy-start | bytes 49156
  4.5 0.7 %copy-start.5 = (f32[4,8,128]{2,1,0:T(8,128)S(1)}, f32[4,8,128]{2,1,0:T(8,128)}, u32[]{:S(2)}) copy-start(f32[4,8,128]{2,1,0:T(8,128)} %refs_3_.1) | copy-start | bytes 49156
  5.2 0.7 %copy-start.6 = (f32[4,8,128]{2,1,0:T(8,128)S(1)}, f32[4,8,128]{2,1,0:T(8,128)}, u32[]{:S(2)}) copy-start(f32[4,8,128]{2,1,0:T(8,128)} %refs_4_.1) | copy-start | bytes 49156
  6.3 1.4 %collective-permute-start.1 = (bf16[5,4,8,128]{3,2,1,0:T(8,128)(2,1)S(1)}, bf16[5,4,8,128]{3,2,1,0:T(8,128)(2,1)S(1)}, u32[]{:S(2)}, u32[]{:S(2)}) collective-permute-start(bf16[5,4,8,128]{3,2,1,0:T(8,128)(2,1)S(1)} %get-tuple-element.12), channel_id=1, source_target_pairs={{0,1},{1,0},{2,3},{3,2},{4,5},{5,4},{6,7},{7,6},{8,9},{9,8},{10,11... | collective-permute-start | bytes 122888 | tf_op jit(solution)/shard_map/ppermute | solution.py:429
  7.8 11.2 %collective-permute-start.7 = (bf16[2,5,4,8,128]{4,3,2,1,0:T(8,128)(2,1)S(1)}, bf16[2,5,4,8,128]{4,3,2,1,0:T(8,128)(2,1)S(1)}, u32[]{:S(2)}, u32[]{:S(2)}) collective-permute-start(bf16[2,5,4,8,128]{4,3,2,1,0:T(8,128)(2,1)S(1)} %bitcast_dynamic-update-slice_fusion.refs_5_), channel_id=1, source_target_pairs={{12,0},{8,4},{4,8},{0,12},{13,1},{9,5},{5,9},{1,13},{14,2},{10,6},... | collective-permute-start | bytes 245768 | tf_op jit(solution)/shard_map/ppermute | solution.py:435
  12.7 7.1 %collective-permute-start.5 = (bf16[2,5,4,8,128]{4,3,2,1,0:T(8,128)(2,1)S(1)}, bf16[2,5,4,8,128]{4,3,2,1,0:T(8,128)(2,1)S(1)}, u32[]{:S(2)}, u32[]{:S(2)}) collective-permute-start(bf16[2,5,4,8,128]{4,3,2,1,0:T(8,128)(2,1)S(1)} %bitcast_dynamic-update-slice_fusion.refs_5_), channel_id=1, source_target_pairs={{8,0},{12,4},{0,8},{4,12},{9,1},{13,5},{1,9},{5,13},{10,2},{14,6},... | collective-permute-start | bytes 245768 | tf_op jit(solution)/shard_map/ppermute | solution.py:435
  12.7 8.6 %collective-permute-start.3 = (bf16[2,5,4,8,128]{4,3,2,1,0:T(8,128)(2,1)S(1)}, bf16[2,5,4,8,128]{4,3,2,1,0:T(8,128)(2,1)S(1)}, u32[]{:S(2)}, u32[]{:S(2)}) collective-permute-start(bf16[2,5,4,8,128]{4,3,2,1,0:T(8,128)(2,1)S(1)} %bitcast_dynamic-update-slice_fusion.refs_5_), channel_id=1, source_target_pairs={{4,0},{0,4},{12,8},{8,12},{5,1},{1,5},{13,9},{9,13},{6,2},{2,6},{1... | collective-permute-start | bytes 245768 | tf_op jit(solution)/shard_map/ppermute | solution.py:435
  13.4 13.4 %copy-start.7 = (f32[4,16]{1,0:T(4,128)S(1)}, f32[4,16]{1,0:T(4,128)}, u32[]{:S(2)}) copy-start(f32[4,16]{1,0:T(4,128)} %refs_0_.3) | copy-start | bytes 772
  13.4 13.4 %copy-start.8 = (s32[4,3]{1,0:T(4,128)S(1)}, s32[4,3]{1,0:T(4,128)}, u32[]{:S(2)}) copy-start(s32[4,3]{1,0:T(4,128)} %refs_1_.3) | copy-start | bytes 148
  15.9 10.9 %copy-start.9 = (f32[32]{0:T(128)S(1)}, f32[32]{0:T(128)}, u32[]{:S(2)}) copy-start(f32[32]{0:T(128)} %param.12) | copy-start | bytes 388
  15.9 6.8 %collective-permute-start = (f32[8,32,128]{2,1,0:T(8,128)S(1)}, f32[8,32,128]{2,1,0:T(8,128)S(1)}, u32[]{:S(2)}, u32[]{:S(2)}) collective-permute-start(f32[8,32,128]{2,1,0:T(8,128)S(1)} %inject.1.refs_3_), channel_id=1, source_target_pairs={{0,1},{2,3},{4,5},{6,7},{8,9},{10,11},{12,13},{14,15},{16,17},{18,... | collective-permute-start | bytes 393224 | tf_op jit(solution)/shard_map/ppermute | solution.py:441
  17.4 5.4 %collective-permute-start.2 = (bf16[2,5,4,8,128]{4,3,2,1,0:T(8,128)(2,1)S(1)}, bf16[2,5,4,8,128]{4,3,2,1,0:T(8,128)(2,1)S(1)}, u32[]{:S(2)}, u32[]{:S(2)}) collective-permute-start(bf16[2,5,4,8,128]{4,3,2,1,0:T(8,128)(2,1)S(1)} %bitcast_dynamic-update-slice_fusion.refs_5_), channel_id=1, source_target_pairs={{0,2},{1,3},{2,0},{3,1},{4,6},{5,7},{6,4},{7,5},{8,10},{9,11},{10,... | collective-permute-start | bytes 245768 | tf_op jit(solution)/shard_map/ppermute | solution.py:439
  18.9 5.6 %collective-permute-start.8 = (bf16[2,5,4,8,128]{4,3,2,1,0:T(8,128)(2,1)S(1)}, bf16[2,5,4,8,128]{4,3,2,1,0:T(8,128)(2,1)S(1)}, u32[]{:S(2)}, u32[]{:S(2)}) collective-permute-start(bf16[2,5,4,8,128]{4,3,2,1,0:T(8,128)(2,1)S(1)} %collective-permute-done.7.refs_11_), channel_id=1, source_target_pairs={{0,2},{1,3},{2,0},{3,1},{4,6},{5,7},{6,4},{7,5},{8,10},{9,11},{10,... | collective-permute-start | bytes 245768 | tf_op jit(solution)/shard_map/ppermute | solution.py:439
  19.9 6.0 %collective-permute-start.6 = (bf16[2,5,4,8,128]{4,3,2,1,0:T(8,128)(2,1)S(1)}, bf16[2,5,4,8,128]{4,3,2,1,0:T(8,128)(2,1)S(1)}, u32[]{:S(2)}, u32[]{:S(2)}) collective-permute-start(bf16[2,5,4,8,128]{4,3,2,1,0:T(8,128)(2,1)S(1)} %collective-permute-done.5.refs_9_), channel_id=1, source_target_pairs={{0,2},{1,3},{2,0},{3,1},{4,6},{5,7},{6,4},{7,5},{8,10},{9,11},{10,... | collective-permute-start | bytes 245768 | tf_op jit(solution)/shard_map/ppermute | solution.py:439
  21.4 5.4 %collective-permute-start.4 = (bf16[2,5,4,8,128]{4,3,2,1,0:T(8,128)(2,1)S(1)}, bf16[2,5,4,8,128]{4,3,2,1,0:T(8,128)(2,1)S(1)}, u32[]{:S(2)}, u32[]{:S(2)}) collective-permute-start(bf16[2,5,4,8,128]{4,3,2,1,0:T(8,128)(2,1)S(1)} %collective-permute-done.3.refs_7_), channel_id=1, source_target_pairs={{0,2},{1,3},{2,0},{3,1},{4,6},{5,7},{6,4},{7,5},{8,10},{9,11},{10,... | collective-permute-start | bytes 245768 | tf_op jit(solution)/shard_map/ppermute | solution.py:439
  34.0 1.4 %copy-start.10 = (s32[32]{0:T(128)S(1)}, s32[32]{0:T(128)}, u32[]{:S(2)}) copy-start(s32[32]{0:T(128)} %lag_ref.1) | copy-start | bytes 388
  34.0 1.4 %collective-permute-start.9 = (f32[4,6,8,128]{3,2,1,0:T(8,128)S(1)}, f32[4,6,8,128]{3,2,1,0:T(8,128)S(1)}, u32[]{:S(2)}, u32[]{:S(2)}) collective-permute-start(f32[4,6,8,128]{3,2,1,0:T(8,128)S(1)} %get-tuple-element.14), channel_id=1, source_target_pairs={{0,1},{1,0},{2,3},{3,2},{4,5},{5,4},{6,7},{7,6},{8,9},{9,8},{10,11... | collective-permute-start | bytes 294920 | tf_op jit(solution)/shard_map/ppermute | solution.py:445
